TPU v7x, 512 devices: a whole 4x8x8 slice. The times are simulated.
512 devices in a mesh: pos: 64 (over z, y_lo, x), head: 8 (over y_hi, core).
Axes of the slice: x: 4, y: 8 (y_hi: 4, y_lo: 2; y = y_hi * 2 + y_lo), z: 8, core: 2. Of those that a mesh axis runs over, the one named last changes fastest.
Arguments:
- token_ids: int32 [65536], P('pos'), may hold values from 0 to 255
- token_table: float32 [256, 1024], replicated, may hold values from -6 to 6
- row_table: float32 [256, 1024], replicated, may hold values from -6 to 6
- col_table: float32 [256, 1024], replicated, may hold values from -6 to 6
- chan_table: float32 [3, 1024], replicated, may hold values from -6 to 6
- w_query: float32 [1024, 1024], P(None, 'head'), as said below
- w_key: float32 [1024, 1024], P(None, 'head'), as said below
- w_value: float32 [1024, 1024], P(None, 'head'), may hold values from -0.1875 to 0.1875
- w_out: float32 [1024, 1024], P('head', 'pos'), may hold values from -0.1875 to 0.1875
- w_in: float32 [1024, 4096], P('pos', 'head'), may hold values from -0.1875 to 0.1875
- w_down: float32 [4096, 1024], P('head', 'pos'), may hold values from -0.09375 to 0.09375
Outputs:
- latent_out: float32 [512, 1024], P('pos')
Inputs may be any that keep to these rules, and one draw needn't show every extreme that they name: `w_query`: entries of order 1024^-0.5 times a few. `w_key`: entries of order 1024^-0.5 times a few, or larger.
All inputs are finite; a program needn't handle non-finite values.
Results may differ from a plain program's by a relative error of at most 0.0003.
Values sent between devices are 32-bit elements; how exact they have to be, the bound alone decides.
No kernel may reach another device: no remote copies, remote signals or barrier semaphores. Data moves between devices by JAX's collectives and lax.ppermute only.
A program may use at most 128 MiB of HBM per device.

v0:
```python
import jax
import jax.numpy as jnp
from jax import lax
from jax.sharding import PartitionSpec as P

HD = 64
IMG = 256
LAT = 512


def broadcast(shard, axis, root):
    mine = lax.axis_index(axis) == root
    return lax.psum(jnp.where(mine, shard, jnp.zeros_like(shard)), axis)


def combined_all(value, axis, join):
    pieces = jax.tree.map(lambda part: lax.all_gather(part, axis), value)
    head = jax.tree.map(lambda part: part[0], pieces)
    tail = jax.tree.map(lambda part: part[1:], pieces)
    so_far, _ = lax.scan(lambda so_far, piece: (join(so_far, piece), None), head, tail)
    return so_far


def layer_norm(values):
    center = values - jnp.mean(values, axis=-1, keepdims=True)
    spread = jnp.mean(center * center, axis=-1, keepdims=True)
    return center * lax.rsqrt(spread + 1e-05)


def embed(ids, where, tables):
    token_table, row_table, col_table, chan_table = tables
    channel = where % 3
    pixel = where // 3
    summed = jnp.take(token_table, ids, axis=0) + jnp.take(row_table, pixel // IMG, axis=0)
    summed = (
        summed + jnp.take(col_table, pixel % IMG, axis=0) + jnp.take(chan_table, channel, axis=0)
    )
    return layer_norm(summed)


def merge_states(first, second):
    peak = jnp.maximum(first[0], second[0])
    left = jnp.exp(first[0] - peak)
    right = jnp.exp(second[0] - peak)
    weight = first[1] * left + second[1] * right
    accum = first[2] * left[..., None] + second[2] * right[..., None]
    return (peak, weight, accum)


def head_sum(partial_value):
    return lax.psum(partial_value, "head")


def per_device(
    token_ids,
    token_table,
    row_table,
    col_table,
    chan_table,
    w_query,
    w_key,
    w_value,
    w_out,
    w_in,
    w_down,
):
    highest = lax.Precision.HIGHEST
    tables = (token_table, row_table, col_table, chan_table)
    local = token_ids.shape[0]
    n_pos = lax.axis_size("pos")
    index = lax.axis_index("pos")
    total = local * n_pos
    heads_dev = w_key.shape[1] // HD
    key_block = min(512, local)
    lat_pos = total - LAT + jnp.arange(LAT)
    own_queries = jnp.dot(
        embed(token_ids[local - LAT :], lat_pos, tables), w_query, precision=highest
    )
    queries = broadcast(own_queries, "pos", n_pos - 1)
    queries = queries.reshape(LAT, heads_dev, HD).transpose(1, 0, 2) * HD ** (-0.5)

    def step(carry, start):
        top, weight, accum = carry
        where = index * local + start + jnp.arange(key_block)
        ids = lax.dynamic_slice_in_dim(token_ids, start, key_block)
        emb = embed(ids, where, tables)
        keys = jnp.dot(emb, w_key, precision=highest).reshape(key_block, heads_dev, HD)
        vals = jnp.dot(emb, w_value, precision=highest).reshape(key_block, heads_dev, HD)
        scores = jnp.einsum("hld,khd->hlk", queries, keys, precision=highest)
        scores = jnp.where(where[None, None, :] <= lat_pos[None, :, None], scores, -1e30)
        new_top = jnp.maximum(top, jnp.max(scores, axis=-1))
        factor = jnp.exp(top - new_top)
        probs = jnp.exp(scores - new_top[..., None])
        weight = weight * factor + jnp.sum(probs, axis=-1)
        accum = accum * factor[..., None] + jnp.einsum(
            "hlk,khd->hld", probs, vals, precision=highest
        )
        return ((new_top, weight, accum), None)

    starts = jnp.arange(local // key_block) * key_block
    init = (
        jnp.full((heads_dev, LAT), -1e30, jnp.float32),
        jnp.zeros((heads_dev, LAT), jnp.float32),
        jnp.zeros((heads_dev, LAT, HD), jnp.float32),
    )
    (top, weight, accum), _ = lax.scan(step, init, starts)
    lat_rows = LAT // n_pos
    top, weight, accum = combined_all((top, weight, accum), "pos", merge_states)
    weight = lax.dynamic_slice_in_dim(weight, index * lat_rows, lat_rows, 1)
    accum = lax.dynamic_slice_in_dim(accum, index * lat_rows, lat_rows, 1)
    attended = (accum / weight[..., None]).transpose(1, 0, 2).reshape(lat_rows, heads_dev * HD)
    whole_out, whole_in, whole_down = (
        lax.all_gather(w_out, "pos", axis=1, tiled=True),
        lax.all_gather(w_in, "pos", axis=0, tiled=True),
        lax.all_gather(w_down, "pos", axis=1, tiled=True),
    )
    projected = head_sum(jnp.dot(attended, whole_out, precision=highest))
    hidden = jax.nn.gelu(jnp.dot(layer_norm(projected), whole_in, precision=highest))
    return projected + head_sum(jnp.dot(hidden, whole_down, precision=highest))


def solution(mesh):
    placed = (
        P("pos"),
        P(),
        P(),
        P(),
        P(),
        P(None, "head"),
        P(None, "head"),
        P(None, "head"),
        P("head", "pos"),
        P("pos", "head"),
        P("head", "pos"),
    )
    return jax.shard_map(
        per_device, mesh=mesh, in_specs=placed, out_specs=P("pos", None), check_vma=False
    )
```

profile of v0, /device:TPU:1, one launch (start us, length us, event | category | flops | bytes accessed | tf_op | source)
XLA Modules:
  0.0 1642.1 jit_solution(15092672931124769)
XLA Ops:
  8.1 4.9 gather_fusion.4
  13.1 2.7 gather_fusion.5
  15.8 2.7 gather_fusion.6
  18.4 2.6 gather_fusion.7
  21.1 4.0 fusion.61
  25.1 1.3 copy-done.7
  26.8 4.3 fusion.34
  31.2 540.8 %all-reduce.2.cloned.1.call-done = f32[512,128]{1,0:T(8,128)} async-done(((f32[512,128]{1,0:T(8,128)}), f32[512,128]{1,0:T(8,128)}) %all-reduce.2.cloned.1.call-update) | async-done | bytes 262160 | tf_op jit(solution)/shard_map/psum | solution.py:13
  573.1 72.5 %while.33 = (s32[]{:T(128)}, f32[2,512]{1,0:T(2,128)S(1)}, f32[2,512]{1,0:T(2,128)S(1)}, f32[2,512,64]{1,2,0:T(8,128)}, s32[2]{0:T(128)S(1)}, /*index=5*/s32[]{:...) while((s32[]{:T(128)}, f32[2,512]{1,0:T(2,128)S(1)}, ...), condition=%wide.region_8.11_spmd.clone, body=%wide.region_3.0_spmd.clone.sunk | while | flops 2427988480 | bytes 55456068 | solution.py:106
  576.7 2.7 gather_fusion.3
  579.4 2.6 gather_fusion
  582.1 4.8 gather_fusion.1
  586.9 2.7 gather_fusion.2
  589.7 4.0 fusion.101
  594.7 3.2 fusion.107
  597.9 2.5 fusion.102
  600.7 3.4 fusion.103
  604.0 2.2 fusion.105
  606.4 2.6 fusion.108
  612.4 2.7 gather_fusion.3
  615.1 2.6 gather_fusion
  617.8 4.8 gather_fusion.1
  622.6 2.7 gather_fusion.2
  625.4 4.0 fusion.101
  630.4 3.2 fusion.107
  633.6 2.5 fusion.102
  636.3 3.4 fusion.103
  639.7 2.2 fusion.105
  642.0 3.6 fusion.108
  646.9 133.4 %all_gather.33 = f32[128,1024]{0,1:T(8,128)S(1)} all-gather(f32[128,16]{0,1:T(8,128)S(1)} %copy-done.12), channel_id=1, replica_groups=mesh['pos'=64,'head'=8] {'pos'}, dimensions={1}, use_global_device_ids=true | all-gather | bytes 532480 | tf_op jit(solution)/shard_map/all_gather | solution.py:113
  780.4 131.1 %all-gather.4 = f32[64,2,512]{2,1,0:T(2,128)S(1)} all-gather(f32[1,2,512]{2,1,0:T(2,128)S(1)} %bitcast.83), channel_id=3, replica_groups=mesh['pos'=64,'head'=8] {'pos'}, dimensions={0}, use_global_device_ids=true | all-gather | bytes 266240 | tf_op jit(solution)/shard_map/all_gather | solution.py:17
  911.5 130.9 %all-gather.3 = f32[64,2,512]{2,1,0:T(2,128)S(1)} all-gather(f32[1,2,512]{2,1,0:T(2,128)S(1)} %bitcast.82), channel_id=2, replica_groups=mesh['pos'=64,'head'=8] {'pos'}, dimensions={0}, use_global_device_ids=true | all-gather | bytes 266240 | tf_op jit(solution)/shard_map/all_gather | solution.py:17
  1043.6 12.2 slice.59
  1055.8 106.7 %while.32 = (s32[]{:T(128)}, f32[2,512]{1,0:T(2,128)S(1)}, f32[2,512]{1,0:T(2,128)S(1)}, f32[2,512,64]{2,1,0:T(8,128)S(1)}, f32[63,2,512]{2,1,0:T(2,128)S(1)}, /...) while((s32[]{:T(128)}, f32[2,512]{1,0:T(2,128)S(1)}, f32[2,512]{1,0:T(2,128)S(1)}, ...), condition=%wide.region_10.13_spmd, body=%wide.region_9.12_spmd.sunk | while | flops 202754 | bytes 1876061 | solution.py:20
  1057.5 1.0 constant_dynamic-slice_fusion.3
  1059.2 1.0 constant_dynamic-slice_fusion.3
  1060.9 1.0 constant_dynamic-slice_fusion.3
  1062.6 1.0 constant_dynamic-slice_fusion.3
  1064.3 1.0 constant_dynamic-slice_fusion.3
  1066.0 1.0 constant_dynamic-slice_fusion.3
  1071.1 1.0 constant_dynamic-slice_fusion.3
  1072.8 1.0 constant_dynamic-slice_fusion.3
  1074.5 1.0 constant_dynamic-slice_fusion.3
  1076.2 1.0 constant_dynamic-slice_fusion.3
  1077.8 1.0 constant_dynamic-slice_fusion.3
  1079.5 1.0 constant_dynamic-slice_fusion.3
  1081.2 1.0 constant_dynamic-slice_fusion.3
  1082.9 1.0 constant_dynamic-slice_fusion.3
  1084.6 1.0 constant_dynamic-slice_fusion.3
  1086.3 1.0 constant_dynamic-slice_fusion.3
  1091.4 1.0 constant_dynamic-slice_fusion.3
  1093.1 1.0 constant_dynamic-slice_fusion.3
  1111.7 1.0 constant_dynamic-slice_fusion.3
  1118.5 1.0 constant_dynamic-slice_fusion.3
  1120.2 1.0 constant_dynamic-slice_fusion.3
  1127.0 1.0 constant_dynamic-slice_fusion.3
  1135.4 1.0 constant_dynamic-slice_fusion.3
  1137.1 1.0 constant_dynamic-slice_fusion.3
  1145.6 1.0 constant_dynamic-slice_fusion.3
  1163.2 119.5 %psum.22 = f32[8,1024]{1,0:T(8,128)S(1)} all-reduce(f32[8,1024]{1,0:T(8,128)S(1)} %fusion.62), channel_id=1, replica_groups=mesh['pos'=64,'head'=8] {'head'}, use_global_device_ids=true, to_apply=%region_11.14 | all-reduce | flops 8192 | bytes 65536 | tf_op jit(solution)/shard_map/psum | solution.py:51
  1283.2 2.8 fusion.48
  1285.9 275.1 %all-gather.11.cloned.1.call-done = f32[512,1024]{0,1:T(8,128)} async-done(((f32[512,16]{0,1:T(8,128)}), f32[512,1024]{0,1:T(8,128)}) %all-gather.11.cloned.1.call-update) | async-done | bytes 2097168 | tf_op jit(solution)/shard_map/all_gather | solution.py:115
  1561.0 3.4 fusion.63
  1564.4 70.6 %psum.23 = f32[8,1024]{1,0:T(8,128)S(1)} all-reduce(f32[8,1024]{1,0:T(8,128)S(1)} %fusion.63), channel_id=1, replica_groups=mesh['pos'=64,'head'=8] {'head'}, use_global_device_ids=true, to_apply=%region_14.17 | all-reduce | flops 8192 | bytes 65536 | tf_op jit(solution)/shard_map/psum | solution.py:51
  (337 shorter events, 92.2 us)
Async XLA Ops:
  6.5 20.2 %copy-start = (f32[1024,128]{1,0:T(8,128)S(1)}, f32[1024,128]{1,0:T(8,128)}, u32[]{:S(2)}) copy-start(f32[1024,128]{1,0:T(8,128)} %param.24) | copy-start | bytes 1572868
  6.5 565.4 %all-reduce.2.cloned.1.call-start = ((), (), s32[]{:S(2)}) async-start(), calls=%async_computation | async-start | bytes 524288 | tf_op jit(solution)/shard_map/psum | solution.py:13
  8.1 5.0 copy-start.4
  13.1 2.7 copy-start.5
  15.8 2.7 copy-start.2
  25.0 1.3 copy-start.7
  26.7 546.3 %copy-start.3 = (f32[256,1024]{1,0:T(8,128)S(1)}, f32[256,1024]{1,0:T(8,128)}, u32[]{:S(2)}) copy-start(f32[256,1024]{1,0:T(8,128)} %param.20) | copy-start | bytes 3145732
  26.8 546.3 %copy-start.8 = (f32[1024,128]{1,0:T(8,128)S(1)}, f32[1024,128]{1,0:T(8,128)}, u32[]{:S(2)}) copy-start(f32[1024,128]{1,0:T(8,128)} %param.25) | copy-start | bytes 1572868
  26.8 546.3 %copy-start.11 = (s32[1024]{0:T(1024)S(1)}, s32[1024]{0:T(1024)}, u32[]{:S(2)}) copy-start(s32[1024]{0:T(1024)} %param.19) | copy-start | bytes 12292
  31.1 1011.4 %all-gather.13.cloned.1.call-start = ((), (), s32[]{:S(2)}) async-start(), calls=%async_computation.3 | async-start | bytes 17039360 | tf_op jit(solution)/shard_map/all_gather | solution.py:17
  573.1 73.9 %copy-start.12 = (f32[128,16]{0,1:T(8,128)S(1)}, f32[128,16]{0,1:T(8,128)}, u32[]{:S(2)}) copy-start(f32[128,16]{0,1:T(8,128)} %param.27) | copy-start | bytes 24580
  593.6 1.0 copy-start.9
  604.0 2.2 copy-start.10
  604.0 2.3 copy-start.6
  629.3 1.0 copy-start.9
  639.7 2.2 copy-start.10
  639.7 2.3 copy-start.6
  645.6 637.5 %all-gather.9.cloned.1.call-start = ((), (), s32[]{:S(2)}) async-start(), calls=%async_computation.1 | async-start | bytes 2129920 | tf_op jit(solution)/shard_map/all_gather | solution.py:114
  646.4 914.6 %all-gather.11.cloned.1.call-start = ((), (), s32[]{:S(2)}) async-start(), calls=%async_computation.2 | async-start | bytes 2129920 | tf_op jit(solution)/shard_map/all_gather | solution.py:115
  1283.1 352.5 %copy-start.1 = (f32[1024,128]{1,0:T(8,128)S(1)}, f32[1024,128]{1,0:T(8,128)}, u32[]{:S(2)}) copy-start(f32[1024,128]{1,0:T(8,128)} %param.24) | copy-start | bytes 1572868
Sparse Core Ops, SparseCore 0:
  31.2 540.6 all-reduce.1
  645.7 318.9 all-gather.12
  966.8 292.8 all-gather.8
  1261.7 299.2 all-gather.10
where the time goes:
time: 1650 us; the launch traced here: 1640 us
  waiting for transfers between devices  817 us (50%)
  blocking collectives  586 us (36%)
  local copies, waits for them, and re-layouts  130 us (8%)
  other arithmetic  52.8 us (3%)
  matrix products  35.3 us (2%)
    psum x1, waiting for transfers between devices, broadcast(): return lax.psum(jnp.where(mine, shard, jnp.zeros_like(shard)), axis)  541 us
    all_gather x1, waiting for transfers between devices, per_device(): lax.all_gather(w_down, 'pos', axis=1, tiled=True)  275 us
    all_gather x2, blocking collectives, combined_all(): pieces = jax.tree.map(lambda part: lax.all_gather(part, axis), value)  262 us
    psum x2, blocking collectives, head_sum(): return lax.psum(partial_value, 'head')  190 us
    all_gather x1, blocking collectives, per_device(): lax.all_gather(w_out, 'pos', axis=1, tiled=True)  133 us
    dynamic_slice x126, local copies, waits for them, and re-layouts, combined_all(): lax.scan(lambda so_far, piece: (join(so_far, piece), None), head, tail)  73.7 us
  transfers between devices with their start and end apart: 4, of which 2 were waited for; matrix products, arithmetic and copies ran while one was open for 7% of the time, Pallas kernels for 0%

commit v1 on v0

v1 whole, which is shorter than its diff:
```python
import functools

import jax
import jax.numpy as jnp
import numpy as np
from jax import lax
from jax.experimental import pallas as pl
from jax.experimental.pallas import tpu as pltpu
from jax.sharding import Mesh
from jax.sharding import PartitionSpec as P

D = 1024
HD = 64
IMG = 256
LAT = 512
POS_DEV = 1024
POSITIONS = 65536
VOCAB = 256
COL_AT = VOCAB
ROW_AT = COL_AT + IMG
ROWS_USED = 88
CHAN_AT = ROW_AT + ROWS_USED
STACK = 640

POS = ("z", "ylo", "x")
HEAD = ("yhi", "core")
PLANE = ("ylo", "x", "yhi", "core")

HIGHEST = lax.Precision.HIGHEST
NT = (((1,), (1,)), ((), ()))
NN = (((1,), (0,)), ((), ()))


def split_tables(token, row, col, chan, parts):
    def put(at, values):
        size = values.shape[0]
        for part in parts:
            rounded = values.astype(jnp.bfloat16)
            part[pl.ds(at, size), :] = rounded
            values = values - rounded.astype(jnp.float32)

    for block in range(2):
        put(block * 128, token[pl.ds(block * 128, 128), :])
        put(COL_AT + block * 128, col[pl.ds(block * 128, 128), :])
    tail = jnp.concatenate(
        [row[pl.ds(0, ROWS_USED), :], chan[...], jnp.zeros((128 - ROWS_USED - 3, D), jnp.float32)],
        axis=0,
    )
    put(ROW_AT, tail)


def embed(ids, first, parts):
    rows = ids.shape[0]
    base = first // 3
    step = lax.broadcasted_iota(jnp.int32, (rows, 1), 0) + (first - base * 3)
    third = (step * 21846) >> 16
    channel = step - third * 3
    pixel = base + third
    lane = lax.broadcasted_iota(jnp.int32, (rows, 256), 1)
    lane_tail = lax.broadcasted_iota(jnp.int32, (rows, 128), 1)

    def hot(mask):
        return jnp.where(mask, 1.0, 0.0).astype(jnp.bfloat16)

    tail = (lane_tail == (pixel >> 8)) | (lane_tail == channel + ROWS_USED)
    picks = jnp.concatenate([hot(lane == ids), hot(lane == (pixel & 255)), hot(tail)], axis=1)
    total = None
    for part in reversed(parts):
        piece = lax.dot_general(picks, part[...], NN, preferred_element_type=jnp.float32)
        total = piece if total is None else total + piece
    center = total - jnp.mean(total, axis=-1, keepdims=True)
    spread = jnp.mean(center * center, axis=-1, keepdims=True)
    return center * lax.rsqrt(spread + 1e-05)


def keys_kernel(index, ids, token, row, col, chan, w_key, w_value, keys, values, *parts):
    block = pl.program_id(0)

    @pl.when(block == 0)
    def _():
        split_tables(token, row, col, chan, parts)

    size = ids.shape[0]
    emb = embed(ids[...], index[0] * POS_DEV + block * size, parts)
    keys[...] = jnp.dot(emb, w_key[...], precision=HIGHEST)
    values[...] = jnp.dot(emb, w_value[...], precision=HIGHEST)


def attend_kernel(index, ids, token, row, col, chan, w_query, keys, values, out, *parts):
    block = pl.program_id(0)

    @pl.when(block == 0)
    def _():
        split_tables(token, row, col, chan, parts)

    size = ids.shape[0]
    first = POSITIONS - LAT + block * size
    emb = embed(ids[...], first, parts)
    queries = jnp.dot(emb, w_query[...], precision=HIGHEST) * HD ** (-0.5)
    low = lax.broadcasted_iota(jnp.int32, (size, 2 * HD), 1) < HD
    low_keys = lax.broadcasted_iota(jnp.int32, (POS_DEV, 2 * HD), 1) < HD
    where = index[0] * POS_DEV + lax.broadcasted_iota(jnp.int32, (size, POS_DEV), 1)
    latent = first + lax.broadcasted_iota(jnp.int32, (size, POS_DEV), 0)
    seen = where <= latent
    tops, weights, accum = [], [], None
    for head in range(2):
        own = low if head == 0 else ~low
        own_values = low_keys if head == 0 else ~low_keys
        scores = lax.dot_general(
            jnp.where(own, queries, 0.0), keys[...], NT, precision=HIGHEST,
            preferred_element_type=jnp.float32,
        )
        scores = jnp.where(seen, scores, -1e30)
        top = jnp.max(scores, axis=-1, keepdims=True)
        probs = jnp.exp(scores - top)
        tops.append(top)
        weights.append(jnp.sum(probs, axis=-1, keepdims=True))
        part = jnp.dot(probs, jnp.where(own_values, values[...], 0.0), precision=HIGHEST)
        accum = part if accum is None else accum + part
    weight = jnp.where(low, weights[0], weights[1])
    top = jnp.where(low, tops[0], tops[1])
    out[:, 0:8, :] = (accum / weight).reshape(size // 8, 8, 2 * HD)
    out[:, 8:16, :] = (top + jnp.log(weight)).reshape(size // 8, 8, 2 * HD)


def project_kernel(states, weights, out):
    level = states[:, 8:16, :]
    share = jnp.exp(level - jnp.max(level, axis=0, keepdims=True))
    attended = jnp.sum(share * states[:, 0:8, :], axis=0) / jnp.sum(share, axis=0)
    for c in range(8):
        block = weights[c * 8 : (c + 1) * 8, 0:16, :].reshape(128, 128)
        out[pl.ds(c, 8, stride=8), :] = lax.dot_general(
            attended, block, NT, precision=HIGHEST, preferred_element_type=jnp.float32
        )


def latent_kernel(rows, weights, out):
    pieces = [rows[pl.ds(c, 64, stride=8), :] for c in range(8)]
    mean = sum(jnp.sum(p, axis=-1, keepdims=True) for p in pieces) * (1.0 / D)
    pieces = [p - mean for p in pieces]
    spread = sum(jnp.sum(p * p, axis=-1, keepdims=True) for p in pieces) * (1.0 / D)
    scale = lax.rsqrt(spread + 1e-05)
    hidden = None
    blocks = []
    for c in range(8):
        block = weights[c * 8 : (c + 1) * 8, 16:32, :].reshape(128, 128)
        blocks.append(block)
        part = jnp.dot(pieces[c] * scale, block, precision=HIGHEST)
        hidden = part if hidden is None else hidden + part
    hidden = jax.nn.gelu(pltpu.roll(hidden, 64, 1))
    lane = lax.broadcasted_iota(jnp.int32, hidden.shape, 1)
    hidden = jnp.where(lane >= 64, hidden, 0.0)
    for c in range(8):
        out[pl.ds(c, 64, stride=8), :] = lax.dot_general(
            hidden, blocks[c], NT, precision=HIGHEST, preferred_element_type=jnp.float32
        )


VMEM = pl.BlockSpec(memory_space=pltpu.VMEM)
SMEM = pl.BlockSpec(memory_space=pltpu.SMEM)


def shape(*dims):
    return jax.ShapeDtypeStruct(dims, jnp.float32)


def params(**more):
    return pltpu.CompilerParams(vmem_limit_bytes=56 * 1024 * 1024, **more)


def exchange(value, axes):
    return lax.all_to_all(value, axes, 0, 0)


def per_device(token_ids, token_table, row_table, col_table, chan_table, w_query, w_key, w_value, w_out, w_in, w_down):
    index = lax.axis_index(POS).astype(jnp.int32).reshape(1)
    tables = (token_table, row_table, col_table, chan_table)

    with jax.named_scope("ids"):
        sent = jnp.broadcast_to(token_ids[POS_DEV - LAT :].reshape(1, 4, 128), (64, 4, 128))
        latent_ids = exchange(sent, POS)[63].reshape(LAT, 1)

    with jax.named_scope("weights"):
        own_out = jnp.broadcast_to(w_out.T.reshape(1, 16, 128), (8, 16, 128))
        own_in = w_in.reshape(16, 8, 64).transpose(1, 0, 2)
        own_down = w_down.reshape(8, 64, 16).transpose(0, 2, 1)
        packed = jnp.concatenate([own_out, jnp.concatenate([own_in, own_down], axis=2)], axis=1)
        packed = jnp.broadcast_to(packed[None], (8, 8, 32, 128)).reshape(64, 32, 128)
        packed, latent_ids = lax.optimization_barrier((packed, latent_ids))
        weights = exchange(packed, POS)

    block = 256
    whole = lambda i: (0, 0)
    table_specs = [
        pl.BlockSpec((VOCAB, D), whole),
        pl.BlockSpec((IMG, D), whole),
        pl.BlockSpec((IMG, D), whole),
        pl.BlockSpec((3, D), whole),
    ]
    splits = [pltpu.VMEM((STACK, D), jnp.bfloat16)] * 3
    keys, values = pl.pallas_call(
        keys_kernel,
        grid=(POS_DEV // block,),
        in_specs=[SMEM, pl.BlockSpec((block, 1), lambda i: (i, 0)), *table_specs]
        + [pl.BlockSpec((D, 128), whole)] * 2,
        out_specs=[pl.BlockSpec((block, 128), lambda i: (i, 0))] * 2,
        out_shape=[shape(POS_DEV, 128)] * 2,
        scratch_shapes=splits,
        compiler_params=params(),
        cost_estimate=pl.CostEstimate(flops=8 * 10**9, transcendentals=0, bytes_accessed=6 * 10**6),
        name="keys",
    )(index, token_ids.reshape(POS_DEV, 1), *tables, w_key, w_value)

    size = 128
    states = pl.pallas_call(
        attend_kernel,
        grid=(LAT // size,),
        in_specs=[SMEM, pl.BlockSpec((size, 1), lambda i: (i, 0)), *table_specs]
        + [pl.BlockSpec((D, 128), whole)]
        + [pl.BlockSpec((POS_DEV, 128), whole)] * 2,
        out_specs=pl.BlockSpec((size // 8, 16, 128), lambda i: (i, 0, 0)),
        out_shape=shape(64, 16, 128),
        scratch_shapes=splits,
        compiler_params=params(),
        cost_estimate=pl.CostEstimate(flops=10 * 10**9, transcendentals=10**6, bytes_accessed=6 * 10**6),
        name="attend",
    )(index, latent_ids, *tables, w_query, keys, values)

    with jax.named_scope("states"):
        states, weights = lax.optimization_barrier((states, weights))
        states = exchange(states, POS)
    partial_rows = pl.pallas_call(
        project_kernel,
        in_specs=[VMEM, VMEM],
        out_specs=VMEM,
        out_shape=shape(64, 128),
        compiler_params=params(),
        name="project",
    )(states, weights)
    with jax.named_scope("projected"):
        projected = jnp.sum(exchange(partial_rows.reshape(8, 8, 128), HEAD), axis=0)
        rows = exchange(jnp.broadcast_to(projected[None], (64, 8, 128)), PLANE)
    outs = pl.pallas_call(
        latent_kernel,
        in_specs=[VMEM, VMEM],
        out_specs=VMEM,
        out_shape=shape(512, 128),
        compiler_params=params(),
        name="latent",
    )(rows.reshape(512, 128), weights)
    with jax.named_scope("result"):
        own = projected + jnp.sum(exchange(outs.reshape(64, 8, 128), PLANE), axis=0)
        return exchange(jnp.broadcast_to(own[None], (8, 8, 128)), HEAD).reshape(8, D)


def solution(mesh):
    fine = Mesh(mesh.devices.reshape(8, 2, 4, 4, 2), ("z", "ylo", "x", "yhi", "core"))
    placed = (
        P(POS),
        P(),
        P(),
        P(),
        P(),
        P(None, HEAD),
        P(None, HEAD),
        P(None, HEAD),
        P(HEAD, POS),
        P(POS, HEAD),
        P(HEAD, POS),
    )
    return jax.shard_map(
        per_device, mesh=fine, in_specs=placed, out_specs=P(POS, None), check_vma=False
    )
```

time: 1650 us -> 171 us (0.10)
  waiting for transfers between devices: 817 us -> 7.99 us
  blocking collectives: 586 us -> 91.5 us
  local copies, waits for them, and re-layouts: 130 us -> 7.17 us
  other arithmetic: 52.8 us -> 0.17 us
  Pallas kernels: 0 us -> 43.2 us
  matrix products: 35.3 us -> 0 us
  starting transfers between devices: 0.12 us -> 20.1 us
    psum x1 -> x0, waiting for transfers between devices: 541 us -> none  [broadcast(): return lax.psum(jnp.where(mine, shard, jnp.zeros_like(shard)), axis)]
    all_gather x3 -> x0, blocking collectives: 395 us -> none  [the longest x2 262 us: combined_all(): pieces = jax.tree.map(lambda part: lax.all_gather(part, axis), value)]
    all_gather x3 -> x0, waiting for transfers between devices: 275 us -> none  [the longest x1 275 us: per_device(): lax.all_gather(w_down, 'pos', axis=1, tiled=True)]
    psum x2 -> x0, blocking collectives: 190 us -> none  [head_sum(): return lax.psum(partial_value, 'head')]
    all_to_all x0 -> x5, blocking collectives: none -> 91.5 us  [exchange(): return lax.all_to_all(value, axes, 0, 0)]
    dynamic_slice x129 -> x0, local copies, waits for them, and re-layouts: 75.1 us -> none  [the longest x126 73.7 us: combined_all(): lax.scan(lambda so_far, piece: (join(so_far, piece), None), head, tail)]
    pallas_call x0 -> x4, Pallas kernels: none -> 43.2 us  [the longest x1 18.3 us: per_device(): pl.pallas_call(attend_kernel, grid=(LAT // size,), in_specs=[SMEM, pl.Blo...]
    gather x12 -> x0, local copies, waits for them, and re-layouts: 38.6 us -> none  [the longest x3 12.3 us: embed(): jnp.take(col_table, pixel % IMG, axis=0)]
  transfers between devices with their start and end apart: 4 -> 2, of which waited for: 2 -> 1; matrix products, arithmetic and copies ran while one was open for 7% -> 1% of each run, Pallas kernels for 0% -> 21%
where the time goes in v1:
time: 171 us; the launch traced here: 170 us
  blocking collectives  91.5 us (54%)
  Pallas kernels  43.2 us (25%)
  starting transfers between devices  20.1 us (12%)
  waiting for transfers between devices  7.99 us (5%)
  local copies, waits for them, and re-layouts  7.17 us (4%)
    all_to_all x5, blocking collectives, exchange(): return lax.all_to_all(value, axes, 0, 0)  91.5 us
    all_to_all x2, starting transfers between devices, exchange(): return lax.all_to_all(value, axes, 0, 0)  20.1 us
    pallas_call x1, Pallas kernels, per_device(): pl.pallas_call(attend_kernel, grid=(LAT // size,), in_specs=[SMEM, pl.Blo...  18.3 us
    pallas_call x1, Pallas kernels, per_device(): pl.pallas_call(keys_kernel, grid=(POS_DEV // block,), in_specs=[SMEM, pl....  17.3 us
    all_to_all x2, waiting for transfers between devices, exchange(): return lax.all_to_all(value, axes, 0, 0)  7.99 us
    pallas_call x1, Pallas kernels, per_device(): pl.pallas_call(latent_kernel, in_specs=[VMEM, VMEM], out_specs=VMEM, out_...  4.67 us
  transfers between devices with their start and end apart: 2, of which 1 were waited for; matrix products, arithmetic and copies ran while one was open for 1% of the time, Pallas kernels for 21%

profile of v1, /device:TPU:1, one launch (start us, length us, event | category | flops | bytes accessed | tf_op | source)
XLA Modules:
  0.0 170.2 jit_solution(17234302048378406278)
XLA Ops:
  0.0 0.7 slice_bitcast_fusion
  0.7 0.7 broadcast_in_dim.12
  1.4 0.0 copy-start.1
  1.4 15.5 %all-to-all-start = ((s32[64,4,128]{2,1,0:T(4,128)}), s32[64,4,128]{2,1,0:T(4,128)S(1)}, u32[]{:S(2)}, u32[]{:S(2)}) async-start(s32[64,4,128]{2,1,0:T(4,128)} %broadcast_in_dim.12), calls=%async_computation | async-start | bytes 262144 | tf_op jit(solution)/shard_map/ids/all_to_all | solution.py:172
  16.8 0.0 copy-done.1
  16.9 0.0 copy-start.2
  16.9 0.1 reshape.47
  16.9 0.7 copy-done.2
  17.6 0.0 copy-start.4
  17.6 0.1 reshape.48
  17.7 0.6 copy-done.4
  18.3 0.1 maximum_maximum_fusion
  18.4 8.0 %all-to-all-done = s32[64,4,128]{2,1,0:T(4,128)S(1)} async-done(((s32[64,4,128]{2,1,0:T(4,128)}), s32[64,4,128]{2,1,0:T(4,128)S(1)}, u32[]{:S(2)}, u32[]{:S(2)}) %all-to-all-start) | async-done | bytes 131104 | tf_op jit(solution)/shard_map/ids/all_to_all | solution.py:172
  26.4 1.1 broadcast_in_dim.11
  27.5 4.7 %all-to-all-start.1 = ((f32[64,32,128]{2,1,0:T(8,128)}), f32[64,32,128]{2,1,0:T(8,128)S(1)}, u32[]{:S(2)}, u32[]{:S(2)}) async-start(f32[64,32,128]{2,1,0:T(8,128)} %bitcast.4), calls=%async_computation.1 | async-start | bytes 2097152 | tf_op jit(solution)/shard_map/weights/all_to_all | solution.py:172
  32.2 0.0 copy-start.3
  32.2 0.7 copy-done.3
  32.9 1.0 copy.17.ids
  33.9 17.3 %keys.1 = (f32[1024,128]{1,0:T(8,128)}, f32[1024,128]{1,0:T(8,128)}) custom-call(s32[1]{0:T(128)} %bitcast.index, s32[1024,1]{1,0:T(8,128)} %copy.17.ids, f32[256,1024]{1,0:T(8,128)} %token_.3, f32[256,1024]{1,0:T(8,128)} %row.3, f32[256,1024]{1,0:T(8,128)} %col.3, f32[3,1024]{1,0:T(4,128)} %chan.3, f32[1024,128]{1,0:T(8,128)} %w_key.1, f32[1024,128]{1,0:T(8,128)} %w_value.1), custom_call_target="tpu_custom_call" | custom-call | flops 8000000000 | bytes 6000000 | tf_op jit(solution)/shard_map/keys/pallas_call | solution.py:201
  51.2 0.9 copy.18.ids
  52.0 18.3 %attend.1 = f32[64,16,128]{2,1,0:T(8,128)} custom-call(s32[1]{0:T(128)} %bitcast.index, s32[512,1]{1,0:T(8,128)} %copy.18.ids, f32[256,1024]{1,0:T(8,128)} %token_.3, f32[256,1024]{1,0:T(8,128)} %row.3, f32[256,1024]{1,0:T(8,128)} %col.3, f32[3,1024]{1,0:T(4,128)} %chan.3, f32[1024,128]{1,0:T(8,128)} %w_query.1, f32[1024,128]{1,0:T(8,128)} %get-tuple-element.12.keys, ...), custom_call_target="tpu_custom_call" | custom-call | flops 10000000000 | bytes 6000000 | tf_op jit(solution)/shard_map/attend/pallas_call | solution.py:215
  70.3 0.0 all-to-all-done.1.weights
  70.3 0.0 copy-start
  70.3 27.6 %all_to_all.35.states = f32[64,16,128]{2,1,0:T(8,128)} all-to-all(f32[64,16,128]{2,1,0:T(8,128)} %attend.1), channel_id=1, replica_groups=mesh['z'=8,'ylo'=2,'x'=4,'yhi'=4,'core'=2] {'z','ylo','x'}, dimensions={0} | all-to-all | bytes 1048576 | tf_op jit(solution)/shard_map/states/all_to_all | solution.py:172
  97.9 0.0 copy-done
  97.9 3.0 %project.1 = f32[64,128]{1,0:T(8,128)} custom-call(f32[64,16,128]{2,1,0:T(8,128)} %all_to_all.35.states, f32[64,32,128]{2,1,0:T(8,128)} %copy-done), custom_call_target="tpu_custom_call" | custom-call | tf_op jit(solution)/shard_map/project/pallas_call | solution.py:232
  100.9 16.1 %all_to_all.36 = f32[8,8,128]{2,1,0:T(8,128)S(1)} all-to-all(f32[8,8,128]{2,1,0:T(8,128)} %bitcast.22), channel_id=1, replica_groups=mesh['z'=8,'ylo'=2,'x'=4,'yhi'=4,'core'=2] {'yhi','core'}, dimensions={0} | all-to-all | bytes 65536 | tf_op jit(solution)/shard_map/projected/all_to_all | solution.py:172
  117.1 17.7 %all_to_all.37 = f32[64,8,128]{2,1,0:T(8,128)} all-to-all(f32[64,8,128]{2,1,0:T(8,128)S(1)} %broadcast_in_dim.13), channel_id=1, replica_groups=mesh['z'=8,'ylo'=2,'x'=4,'yhi'=4,'core'=2] {'ylo','x','yhi','core'}, dimensions={0} | all-to-all | bytes 524288 | tf_op jit(solution)/shard_map/projected/all_to_all | solution.py:172
  134.8 4.7 %latent.1 = f32[512,128]{1,0:T(8,128)} custom-call(f32[512,128]{1,0:T(8,128)} %bitcast.18, f32[64,32,128]{2,1,0:T(8,128)} %copy-done), custom_call_target="tpu_custom_call" | custom-call | tf_op jit(solution)/shard_map/latent/pallas_call | solution.py:243
  139.5 18.7 %all_to_all.38 = f32[64,8,128]{2,1,0:T(8,128)S(1)} all-to-all(f32[64,8,128]{2,1,0:T(8,128)} %bitcast.19), channel_id=1, replica_groups=mesh['z'=8,'ylo'=2,'x'=4,'yhi'=4,'core'=2] {'ylo','x','yhi','core'}, dimensions={0} | all-to-all | bytes 524288 | tf_op jit(solution)/shard_map/result/all_to_all | solution.py:172
  158.2 0.1 reduce_sum.19
  158.3 11.3 %all_to_all.39 = f32[8,8,128]{2,1,0:T(8,128)S(1)} all-to-all(f32[8,8,128]{2,1,0:T(8,128)S(1)} %broadcast_in_dim.14), channel_id=1, replica_groups=mesh['z'=8,'ylo'=2,'x'=4,'yhi'=4,'core'=2] {'yhi','core'}, dimensions={0} | all-to-all | bytes 65536 | tf_op jit(solution)/shard_map/result/all_to_all | solution.py:172
  169.6 0.6 copy.21
  (7 shorter events, 0.1 us)
Async XLA Ops:
  1.4 15.5 %copy-start.1 = (f32[16,512]{1,0:T(8,128)S(1)}, f32[16,512]{1,0:T(8,128)}, u32[]{:S(2)}) copy-start(f32[16,512]{1,0:T(8,128)} %param.20) | copy-start | bytes 98308
  1.4 25.1 %all-to-all-start = ((s32[64,4,128]{2,1,0:T(4,128)}), s32[64,4,128]{2,1,0:T(4,128)S(1)}, u32[]{:S(2)}, u32[]{:S(2)}) async-start(s32[64,4,128]{2,1,0:T(4,128)} %broadcast_in_dim.12), calls=%async_computation | async-start | bytes 262144 | tf_op jit(solution)/shard_map/ids/all_to_all | solution.py:172
  16.9 0.8 copy-start.2
  17.6 0.7 copy-start.4
  27.5 42.8 %all-to-all-start.1 = ((f32[64,32,128]{2,1,0:T(8,128)}), f32[64,32,128]{2,1,0:T(8,128)S(1)}, u32[]{:S(2)}, u32[]{:S(2)}) async-start(f32[64,32,128]{2,1,0:T(8,128)} %bitcast.4), calls=%async_computation.1 | async-start | bytes 2097152 | tf_op jit(solution)/shard_map/weights/all_to_all | solution.py:172
  32.2 0.7 copy-start.3
  70.3 27.6 %copy-start = (f32[64,32,128]{2,1,0:T(8,128)}, f32[64,32,128]{2,1,0:T(8,128)S(1)}, u32[]{:S(2)}) copy-start(f32[64,32,128]{2,1,0:T(8,128)S(1)} %all-to-all-done.1.weights) | copy-start | bytes 3145732

commit v2 on v1

v2 whole, which is shorter than its diff:
```python
import jax
import jax.numpy as jnp
from jax import lax
from jax.experimental import pallas as pl
from jax.experimental.pallas import tpu as pltpu
from jax.sharding import Mesh
from jax.sharding import PartitionSpec as P

D = 1024
HD = 64
IMG = 256
LAT = 512
POS_DEV = 1024
POSITIONS = 65536
VOCAB = 256
ROWS_USED = 88

POS = ("z", "ylo", "x")
HEAD = ("yhi", "core")
COLUMN = ("ylo", "x")
SHARERS = ("z", "yhi", "core")

HIGHEST = lax.Precision.HIGHEST
NT = (((1,), (1,)), ((), ()))
NN = (((1,), (0,)), ((), ()))


def parts_of(values):
    parts = []
    for _ in range(3):
        rounded = values.astype(jnp.bfloat16)
        parts.append(rounded)
        values = values - rounded.astype(jnp.float32)
    return parts


def store_parts(refs, at, values):
    for ref, part in zip(refs, parts_of(values)):
        ref[pl.ds(at, values.shape[0]), :] = part


def place(first, rows):
    base = first // 3
    step = lax.broadcasted_iota(jnp.int32, (rows, 1), 0) + (first - base * 3)
    third = (step * 21846) >> 16
    return step - third * 3, base + third


def hot(mask):
    return jnp.where(mask, 1.0, 0.0).astype(jnp.bfloat16)


def hot_place(first, rows):
    channel, pixel = place(first, rows)
    lane = lax.broadcasted_iota(jnp.int32, (rows, 256), 1)
    tail = lax.broadcasted_iota(jnp.int32, (rows, 128), 1)
    in_tail = (tail == (pixel >> 8)) | (tail == channel + ROWS_USED)
    return jnp.concatenate([hot(lane == (pixel & 255)), hot(in_tail)], axis=1)


def hot_token(ids):
    return hot(lax.broadcasted_iota(jnp.int32, (ids.shape[0], VOCAB), 1) == ids)


def pick(picks, parts):
    total = None
    for part in reversed(parts):
        piece = lax.dot_general(picks, part, NN, preferred_element_type=jnp.float32)
        total = piece if total is None else total + piece
    return total


def normalized(total):
    center = total - jnp.mean(total, axis=-1, keepdims=True)
    spread = jnp.mean(center * center, axis=-1, keepdims=True)
    return center * lax.rsqrt(spread + 1e-05)


def low_lanes(rows):
    return lax.broadcasted_iota(jnp.int32, (rows, 2 * HD), 1) < HD


def pair(low, first, second, head):
    if head == 0:
        return jnp.where(low, first, pltpu.roll(second, HD, 1))
    return jnp.where(low, pltpu.roll(first, HD, 1), second)


def keys_kernel(index, ids, token, row, col, chan, w_key, w_value, key_cat, value_cat, where_sum, t1, t2, t3, p1, p2, p3):
    block = pl.program_id(0)
    tokens, places = (t1, t2, t3), (p1, p2, p3)

    @pl.when(block == 0)
    def _():
        for at in (0, 128):
            store_parts(tokens, at, token[pl.ds(at, 128), :])
            store_parts(places, at, col[pl.ds(at, 128), :])
        rest = jnp.zeros((128 - ROWS_USED - 3, D), jnp.float32)
        store_parts(places, 256, jnp.concatenate([row[pl.ds(0, ROWS_USED), :], chan[...], rest], axis=0))

    size = ids.shape[0]
    lat_size = where_sum.shape[0]
    where_parts = [p[...] for p in places]
    first = index[0] * POS_DEV + block * size
    total = pick(hot_place(first, size), where_parts) + pick(hot_token(ids[...]), [t[...] for t in tokens])
    emb = normalized(total)
    keys = jnp.dot(emb, w_key[...], precision=HIGHEST)
    values = jnp.dot(emb, w_value[...], precision=HIGHEST)
    low = low_lanes(size)
    k = [part.astype(jnp.float32) for part in parts_of(keys)]
    v = [part.astype(jnp.float32) for part in parts_of(values)]
    ones = jnp.ones_like(values)
    for head in range(2):
        both = pair(low, k[0], k[1], head)
        pieces = [both, both, pair(low, k[2], k[0], head), pair(low, k[2], k[1], head)]
        for i, piece in enumerate(pieces):
            key_cat[head, :, i * 128 : (i + 1) * 128] = piece.astype(jnp.bfloat16)
        tail = jnp.where(low, v[2], ones) if head == 0 else jnp.where(low, ones, v[2])
        value_cat[head, :, 0:128] = pair(low, v[0], v[1], head).astype(jnp.bfloat16)
        value_cat[head, :, 128:256] = tail.astype(jnp.bfloat16)
    where_sum[...] = pick(hot_place(POSITIONS - LAT + block * lat_size, lat_size), where_parts)


def attend_kernel(index, ids, where_sum, t1, t2, t3, w_query, key_cat, value_cat, out, attended):
    block = pl.program_id(0)
    size = ids.shape[0]
    emb = normalized(where_sum[...] + pick(hot_token(ids[...]), [t1[...], t2[...], t3[...]]))
    queries = jnp.dot(emb, w_query[...], precision=HIGHEST) * HD ** (-0.5)
    q = [part.astype(jnp.float32) for part in parts_of(queries)]
    low = low_lanes(size)
    where = index[0] * POS_DEV + lax.broadcasted_iota(jnp.int32, (size, POS_DEV), 1)
    latent = POSITIONS - LAT + block * size + lax.broadcasted_iota(jnp.int32, (size, POS_DEV), 0)
    seen = where <= latent
    sums, weights, tops = [], [], []
    for head in range(2):
        query_cat = jnp.concatenate(
            [pair(low, q[0], q[0], head), pair(low, q[1], q[1], head)]
            + [pair(low, q[0], q[2], head), pair(low, q[1], q[2], head)],
            axis=1,
        ).astype(jnp.bfloat16)
        scores = lax.dot_general(query_cat, key_cat[head], NT, preferred_element_type=jnp.float32)
        scores = jnp.where(seen, scores, -1e30)
        top = jnp.max(scores, axis=-1, keepdims=True)
        probs = jnp.exp(scores - top)
        near = probs.astype(jnp.bfloat16)
        rest = (probs - near.astype(jnp.float32)).astype(jnp.bfloat16)
        value = value_cat[head]
        both = jnp.dot(near, value, preferred_element_type=jnp.float32)
        both = both + jnp.dot(rest, value, preferred_element_type=jnp.float32)
        lead, tail = both[:, :128], both[:, 128:]
        sums.append(lead + pltpu.roll(lead, HD, 1) + tail)
        weights.append(pltpu.roll(tail, HD, 1))
        tops.append(top)
    weight = jnp.where(low, weights[0], weights[1])
    level = jnp.where(low, tops[0], tops[1]) + jnp.log(weight)
    attended[...] = jnp.where(low, sums[0], sums[1]) / weight
    chunks = size // 8
    for r in range(8):
        out[pl.ds(r, chunks, stride=9), :] = attended[pl.ds(r, chunks, stride=8), :]
    level = level.reshape(chunks, 8, 128)
    lane = lax.broadcasted_iota(jnp.int32, level.shape, 2)
    lat = lax.broadcasted_iota(jnp.int32, level.shape, 1)
    out[pl.ds(8, chunks, stride=9), :] = jnp.sum(jnp.where((lane & 7) == lat, level, 0.0), axis=1)


def project_kernel(states, weights, out):
    levels = states[pl.ds(8, 64, stride=9), :]
    low = low_lanes(64)
    rows = []
    for r in range(8):
        level = jnp.where(low, levels[:, r : r + 1], levels[:, HD + r : HD + r + 1])
        share = jnp.exp(level - jnp.max(level, axis=0, keepdims=True))
        value = jnp.sum(share * states[pl.ds(r, 64, stride=9), :], axis=0, keepdims=True)
        rows.append(value / jnp.sum(share, axis=0, keepdims=True))
    attended = jnp.concatenate(rows, axis=0)
    for c in range(8):
        block = weights[:, c * 32 : c * 32 + 16, :].reshape(128, 128)
        out[pl.ds(c, 8, stride=8), :] = lax.dot_general(
            attended, block, NT, precision=HIGHEST, preferred_element_type=jnp.float32
        )


def latent_kernel(rows, weights, out):
    pieces = [rows[pl.ds(c, 64, stride=8), :] for c in range(8)]
    mean = sum(jnp.sum(p, axis=-1, keepdims=True) for p in pieces) * (1.0 / D)
    pieces = [p - mean for p in pieces]
    spread = sum(jnp.sum(p * p, axis=-1, keepdims=True) for p in pieces) * (1.0 / D)
    scale = lax.rsqrt(spread + 1e-05)
    hidden = None
    blocks = []
    for c in range(8):
        block = weights[:, c * 32 + 16 : c * 32 + 32, :].reshape(128, 128)
        blocks.append(block)
        part = jnp.dot(pieces[c] * scale, block, precision=HIGHEST)
        hidden = part if hidden is None else hidden + part
    hidden = jax.nn.gelu(pltpu.roll(hidden, 64, 1))
    lane = lax.broadcasted_iota(jnp.int32, hidden.shape, 1)
    hidden = jnp.where(lane >= 64, hidden, 0.0)
    for c in range(8):
        out[pl.ds(c, 64, stride=8), :] = lax.dot_general(
            hidden, blocks[c], NT, precision=HIGHEST, preferred_element_type=jnp.float32
        )


VMEM = pl.BlockSpec(memory_space=pltpu.VMEM)
SMEM = pl.BlockSpec(memory_space=pltpu.SMEM)


def shape(*dims):
    return jax.ShapeDtypeStruct(dims, jnp.float32)


def params(**more):
    return pltpu.CompilerParams(vmem_limit_bytes=56 * 1024 * 1024, **more)


def exchange(value, axes):
    return lax.all_to_all(value, axes, 0, 0)


def per_device(token_ids, token_table, row_table, col_table, chan_table, w_query, w_key, w_value, w_out, w_in, w_down):
    index = lax.axis_index(POS).astype(jnp.int32).reshape(1)

    with jax.named_scope("weights"):
        own_ids = token_ids[POS_DEV - LAT :].astype(jnp.float32).reshape(4, 128)
        own_ids = jnp.concatenate([own_ids, jnp.zeros((4, 128), jnp.float32)], axis=0)
        own_in = w_in.reshape(16, 8, 64).transpose(1, 0, 2)
        own_down = w_down.reshape(8, 64, 16).transpose(0, 2, 1)
        packed = jnp.concatenate(
            [
                jnp.broadcast_to(w_out.T[None], (8, 16, 128)),
                jnp.concatenate([own_in, own_down], axis=2),
                jnp.broadcast_to(own_ids[None], (8, 8, 128)),
            ],
            axis=1,
        )
        packed = exchange(packed, "z")
        packed = jnp.concatenate([packed[:, :32, :].reshape(256, 128), packed[7, 32:, :]], axis=0)
        weights = exchange(jnp.broadcast_to(packed[None], (8, 264, 128)), COLUMN)
        latent_ids = weights[7, 256:260, :].astype(jnp.int32).reshape(LAT, 1)

    steps = 4
    block, size = POS_DEV // steps, LAT // steps
    bf16 = lambda *dims: jax.ShapeDtypeStruct(dims, jnp.bfloat16)
    whole = lambda *dims: pl.BlockSpec(dims, lambda i: (0,) * len(dims))
    slab = lambda *dims: pl.BlockSpec(dims, lambda i: (i,) + (0,) * (len(dims) - 1))
    middle = lambda *dims: pl.BlockSpec(dims, lambda i: (0, i, 0))
    key_cat, value_cat, where_sum, *tokens = pl.pallas_call(
        keys_kernel,
        grid=(steps,),
        in_specs=[SMEM, slab(block, 1), whole(VOCAB, D), whole(IMG, D), whole(IMG, D), whole(3, D)]
        + [whole(D, 128)] * 2,
        out_specs=[middle(2, block, 512), middle(2, block, 256), slab(size, D)] + [whole(VOCAB, D)] * 3,
        out_shape=[bf16(2, POS_DEV, 512), bf16(2, POS_DEV, 256), shape(LAT, D)] + [bf16(VOCAB, D)] * 3,
        scratch_shapes=[pltpu.VMEM((384, D), jnp.bfloat16)] * 3,
        compiler_params=params(),
        cost_estimate=pl.CostEstimate(flops=8 * 10**9, transcendentals=0, bytes_accessed=10**7),
        name="keys",
    )(index, token_ids.reshape(POS_DEV, 1), token_table, row_table, col_table, chan_table, w_key, w_value)

    states = pl.pallas_call(
        attend_kernel,
        grid=(steps,),
        in_specs=[SMEM, slab(size, 1), slab(size, D)]
        + [whole(VOCAB, D)] * 3
        + [whole(D, 128), whole(2, POS_DEV, 512), whole(2, POS_DEV, 256)],
        out_specs=slab(size // 8 * 9, 128),
        out_shape=shape(64 * 9, 128),
        scratch_shapes=[pltpu.VMEM((size, 128), jnp.float32)],
        compiler_params=params(),
        cost_estimate=pl.CostEstimate(flops=6 * 10**9, transcendentals=10**6, bytes_accessed=10**7),
        name="attend",
    )(index, latent_ids, where_sum, *tokens, w_query, key_cat, value_cat)

    with jax.named_scope("states"):
        states = exchange(states.reshape(64, 1, 1152), POS).reshape(64 * 9, 128)
    partial_rows = pl.pallas_call(
        project_kernel,
        in_specs=[VMEM, VMEM],
        out_specs=VMEM,
        out_shape=shape(64, 128),
        compiler_params=params(),
        name="project",
    )(states, weights)
    with jax.named_scope("projected"):
        projected = jnp.sum(exchange(partial_rows.reshape(8, 8, 128), HEAD), axis=0)
        rows = exchange(jnp.broadcast_to(projected[None], (64, 8, 128)), SHARERS)
    outs = pl.pallas_call(
        latent_kernel,
        in_specs=[VMEM, VMEM],
        out_specs=VMEM,
        out_shape=shape(512, 128),
        compiler_params=params(),
        name="latent",
    )(rows.reshape(512, 128), weights)
    with jax.named_scope("result"):
        own = projected + jnp.sum(exchange(outs.reshape(64, 8, 128), SHARERS), axis=0)
        return exchange(jnp.broadcast_to(own[None], (8, 8, 128)), HEAD).reshape(8, D)


def solution(mesh):
    fine = Mesh(mesh.devices.reshape(8, 2, 4, 4, 2), ("z", "ylo", "x", "yhi", "core"))
    placed = (
        P(POS),
        P(),
        P(),
        P(),
        P(),
        P(None, HEAD),
        P(None, HEAD),
        P(None, HEAD),
        P(HEAD, POS),
        P(POS, HEAD),
        P(HEAD, POS),
    )
    return jax.shard_map(
        per_device, mesh=fine, in_specs=placed, out_specs=P(POS, None), check_vma=False
    )
```

time: 171 us -> 161 us (0.942)
  starting transfers between devices: 20.1 us -> 5.16 us
  blocking collectives: 91.5 us -> 106 us
  waiting for transfers between devices: 7.99 us -> 0.01 us
    all_to_all x2 -> x1, starting transfers between devices: 20.1 us -> 5.16 us  [exchange(): return lax.all_to_all(value, axes, 0, 0)]
    all_to_all x5 -> x6, blocking collectives: 91.5 us -> 106 us  [exchange(): return lax.all_to_all(value, axes, 0, 0)]
    all_to_all x2 -> x1, waiting for transfers between devices: 7.99 us -> 0.01 us  [exchange(): return lax.all_to_all(value, axes, 0, 0)]
    unnamed x11 -> x5, local copies, waits for them, and re-layouts: 2.6 us -> 0.63 us
  transfers between devices with their start and end apart: 2 -> 1, of which waited for: 1 -> 0; matrix products, arithmetic and copies ran while one was open for 1% -> 1% of each run, Pallas kernels for 21% -> 12%
where the time goes in v2:
time: 161 us
  blocking collectives  106 us (66%)
  Pallas kernels  42.7 us (27%)
  local copies, waits for them, and re-layouts  6.24 us (4%)
  starting transfers between devices  5.16 us (3%)
    all_to_all x6, blocking collectives, exchange(): return lax.all_to_all(value, axes, 0, 0)  106 us
    pallas_call x1, Pallas kernels, per_device(): pl.pallas_call(keys_kernel, grid=(steps,), in_specs=[SMEM, slab(block, 1)...  20 us
    pallas_call x1, Pallas kernels, per_device(): pl.pallas_call(attend_kernel, grid=(steps,), in_specs=[SMEM, slab(size, 1...  15 us
    all_to_all x1, starting transfers between devices, exchange(): return lax.all_to_all(value, axes, 0, 0)  5.16 us
    pallas_call x1, Pallas kernels, per_device(): pl.pallas_call(latent_kernel, in_specs=[VMEM, VMEM], out_specs=VMEM, out_...  4.67 us
  transfers between devices with their start and end apart: 1, of which 0 were waited for; matrix products, arithmetic and copies ran while one was open for 1% of the time, Pallas kernels for 12%

profile of v2, /device:TPU:1, one launch (start us, length us, event | category | flops | bytes accessed | tf_op | source)
XLA Modules:
  0.0 160.7 jit_solution(15561044371028994861)
XLA Ops:
  0.0 0.7 convert_bitcast_fusion
  0.7 0.8 reshape.65
  1.5 0.8 reshape.66
  2.4 0.7 broadcast_in_dim.10
  3.1 0.1 pad_maximum_fusion
  3.2 18.9 %all_to_all.35 = f32[8,40,128]{2,1,0:T(8,128)S(1)} all-to-all(f32[8,40,128]{2,1,0:T(8,128)S(1)} %pad_maximum_fusion), channel_id=1, replica_groups=mesh['z'=8,'ylo'=2,'x'=4,'yhi'=4,'core'=2] {'z'}, dimensions={0} | all-to-all | bytes 327680 | tf_op jit(solution)/shard_map/weights/all_to_all | solution.py:218
  22.1 1.0 broadcast_in_dim.12
  23.2 0.0 copy-start.1
  23.2 5.2 %all-to-all-start.1 = ((f32[8,264,128]{2,1,0:T(8,128)}), f32[8,264,128]{2,1,0:T(8,128)S(1)}, u32[]{:S(2)}, u32[]{:S(2)}) async-start(f32[8,264,128]{2,1,0:T(8,128)} %broadcast_in_dim.12), calls=%async_computation.1 | async-start | bytes 2162688 | tf_op jit(solution)/shard_map/weights/all_to_all | solution.py:218
  28.3 0.0 copy-done.1
  28.3 1.1 copy.21.ids
  29.4 20.0 %keys.1 = (bf16[2,1024,512]{2,1,0:T(8,128)(2,1)}, bf16[2,1024,256]{2,1,0:T(8,128)(2,1)}, f32[512,1024]{1,0:T(8,128)}, bf16[256,1024]{1,0:T(8,128)(2,1)}, bf16[25...) custom-call(s32[1]{0:T(128)} %bitcast.index, s32[1024,1]{1,0:T(8,128)} %copy.21.ids, f32[256,1024]{1,0:T(8,128)} %token_.1, ...), custom_call_target="tpu_custom_call" | custom-call | flops 8000000000 | bytes 10000000 | tf_op jit(solution)/shard_map/keys/pallas_call | solution.py:248
  49.4 0.0 all-to-all-done.1.weights
  49.4 0.0 copy-start
  49.4 1.1 copy.22.ids
  50.5 15.0 %attend.1 = f32[576,128]{1,0:T(8,128)} custom-call(s32[1]{0:T(128)} %bitcast.index, s32[512,1]{1,0:T(8,128)} %copy.22.ids, f32[512,1024]{1,0:T(8,128)} %get-tuple-element.11.where_sum, bf16[256,1024]{1,0:T(8,128)(2,1)} %get-tuple-element.12.t1, bf16[256,1024]{1,0:T(8,128)(2,1)} %get-tuple-element.13.t2, bf16[256,1024]{1,0:T(8,128)(2,1)} %get-tuple-element.14.t3, ...), custom_call_target="tpu_custom_call" | custom-call | flops 6000000000 | bytes 10000000 | tf_op jit(solution)/shard_map/attend/pallas_call | solution.py:261
  65.4 0.0 copy-done
  65.4 18.8 %all_to_all.36 = f32[64,1,1152]{2,1,0:T(1,128)} all-to-all(f32[64,1,1152]{2,1,0:T(1,128)} %bitcast.30), channel_id=1, replica_groups=mesh['z'=8,'ylo'=2,'x'=4,'yhi'=4,'core'=2] {'z','ylo','x'}, dimensions={0} | all-to-all | bytes 589824 | tf_op jit(solution)/shard_map/states/all_to_all | solution.py:218
  84.3 3.1 %project.1 = f32[64,128]{1,0:T(8,128)} custom-call(f32[576,128]{1,0:T(8,128)} %bitcast.26, f32[8,264,128]{2,1,0:T(8,128)} %copy-done), custom_call_target="tpu_custom_call" | custom-call | tf_op jit(solution)/shard_map/project/pallas_call | solution.py:277
  87.4 16.8 %all_to_all.37 = f32[8,8,128]{2,1,0:T(8,128)S(1)} all-to-all(f32[8,8,128]{2,1,0:T(8,128)} %bitcast.33), channel_id=1, replica_groups=mesh['z'=8,'ylo'=2,'x'=4,'yhi'=4,'core'=2] {'yhi','core'}, dimensions={0} | all-to-all | bytes 65536 | tf_op jit(solution)/shard_map/projected/all_to_all | solution.py:218
  104.2 20.5 %all_to_all.38 = f32[64,8,128]{2,1,0:T(8,128)} all-to-all(f32[64,8,128]{2,1,0:T(8,128)S(1)} %broadcast_in_dim.13), channel_id=1, replica_groups=mesh['z'=8,'ylo'=2,'x'=4,'yhi'=4,'core'=2] {'z','yhi','core'}, dimensions={0} | all-to-all | bytes 524288 | tf_op jit(solution)/shard_map/projected/all_to_all | solution.py:218
  124.8 4.7 %latent.1 = f32[512,128]{1,0:T(8,128)} custom-call(f32[512,128]{1,0:T(8,128)} %bitcast.27, f32[8,264,128]{2,1,0:T(8,128)} %copy-done), custom_call_target="tpu_custom_call" | custom-call | tf_op jit(solution)/shard_map/latent/pallas_call | solution.py:288
  129.4 20.2 %all_to_all.39 = f32[64,8,128]{2,1,0:T(8,128)S(1)} all-to-all(f32[64,8,128]{2,1,0:T(8,128)} %bitcast.28), channel_id=1, replica_groups=mesh['z'=8,'ylo'=2,'x'=4,'yhi'=4,'core'=2] {'z','yhi','core'}, dimensions={0} | all-to-all | bytes 524288 | tf_op jit(solution)/shard_map/result/all_to_all | solution.py:218
  149.6 0.1 reduce_sum.19
  149.7 10.3 %all_to_all.40 = f32[8,8,128]{2,1,0:T(8,128)S(1)} all-to-all(f32[8,8,128]{2,1,0:T(8,128)S(1)} %broadcast_in_dim.14), channel_id=1, replica_groups=mesh['z'=8,'ylo'=2,'x'=4,'yhi'=4,'core'=2] {'yhi','core'}, dimensions={0} | all-to-all | bytes 65536 | tf_op jit(solution)/shard_map/result/all_to_all | solution.py:218
  160.1 0.6 copy.30
  (12 shorter events, 0.1 us)
Async XLA Ops:
  23.2 5.2 %copy-start.1 = (s32[1024]{0:T(1024)S(1)}, s32[1024]{0:T(1024)}, u32[]{:S(2)}) copy-start(s32[1024]{0:T(1024)} %param.11) | copy-start | bytes 12292
  23.2 26.2 %all-to-all-start.1 = ((f32[8,264,128]{2,1,0:T(8,128)}), f32[8,264,128]{2,1,0:T(8,128)S(1)}, u32[]{:S(2)}, u32[]{:S(2)}) async-start(f32[8,264,128]{2,1,0:T(8,128)} %broadcast_in_dim.12), calls=%async_computation.1 | async-start | bytes 2162688 | tf_op jit(solution)/shard_map/weights/all_to_all | solution.py:218
  49.4 16.1 %copy-start = (f32[8,264,128]{2,1,0:T(8,128)}, f32[8,264,128]{2,1,0:T(8,128)S(1)}, u32[]{:S(2)}) copy-start(f32[8,264,128]{2,1,0:T(8,128)S(1)} %all-to-all-done.1.weights) | copy-start | bytes 3244036

commit v3 on v2

--- a/solution.py
+++ b/solution.py
@@ -14,6 +14,8 @@
 POSITIONS = 65536
 VOCAB = 256
 ROWS_USED = 88
+KEY_STEPS = 2
+LATENT_STEPS = 2
 
 POS = ("z", "ylo", "x")
 HEAD = ("yhi", "core")
@@ -86,26 +88,24 @@
     return jnp.where(low, pltpu.roll(first, HD, 1), second)
 
 
-def keys_kernel(index, ids, token, row, col, chan, w_key, w_value, key_cat, value_cat, where_sum, t1, t2, t3, p1, p2, p3):
-    block = pl.program_id(0)
+def tables_kernel(token, row, col, chan, t1, t2, t3, p1, p2, p3, where_sum):
     tokens, places = (t1, t2, t3), (p1, p2, p3)
-
-    @pl.when(block == 0)
-    def _():
-        for at in (0, 128):
-            store_parts(tokens, at, token[pl.ds(at, 128), :])
-            store_parts(places, at, col[pl.ds(at, 128), :])
-        rest = jnp.zeros((128 - ROWS_USED - 3, D), jnp.float32)
-        store_parts(places, 256, jnp.concatenate([row[pl.ds(0, ROWS_USED), :], chan[...], rest], axis=0))
-
+    for at in (0, 128):
+        store_parts(tokens, at, token[pl.ds(at, 128), :])
+        store_parts(places, at, col[pl.ds(at, 128), :])
+    rest = jnp.zeros((128 - ROWS_USED - 3, token.shape[1]), jnp.float32)
+    store_parts(places, 256, jnp.concatenate([row[...], chan[...], rest], axis=0))
+    where_sum[...] = pick(hot_place(POSITIONS - LAT, LAT), [p[...] for p in places])
+
+
+def keys_kernel(index, ids, t1, t2, t3, p1, p2, p3, w_key, w_value, key_cat, value_cat):
     size = ids.shape[0]
-    lat_size = where_sum.shape[0]
-    where_parts = [p[...] for p in places]
-    first = index[0] * POS_DEV + block * size
-    total = pick(hot_place(first, size), where_parts) + pick(hot_token(ids[...]), [t[...] for t in tokens])
+    first = index[0] * POS_DEV + pl.program_id(0) * size
+    total = pick(hot_place(first, size), [p1[...], p2[...], p3[...]])
+    total = total + pick(hot_token(ids[...]), [t1[...], t2[...], t3[...]])
     emb = normalized(total)
-    keys = jnp.dot(emb, w_key[...], precision=HIGHEST)
-    values = jnp.dot(emb, w_value[...], precision=HIGHEST)
+    both = jnp.dot(emb, jnp.concatenate([w_key[...], w_value[...]], axis=1), precision=HIGHEST)
+    keys, values = both[:, :128], both[:, 128:]
     low = low_lanes(size)
     k = [part.astype(jnp.float32) for part in parts_of(keys)]
     v = [part.astype(jnp.float32) for part in parts_of(values)]
@@ -118,14 +118,24 @@
         tail = jnp.where(low, v[2], ones) if head == 0 else jnp.where(low, ones, v[2])
         value_cat[head, :, 0:128] = pair(low, v[0], v[1], head).astype(jnp.bfloat16)
         value_cat[head, :, 128:256] = tail.astype(jnp.bfloat16)
-    where_sum[...] = pick(hot_place(POSITIONS - LAT + block * lat_size, lat_size), where_parts)
 
 
 def attend_kernel(index, ids, where_sum, t1, t2, t3, w_query, key_cat, value_cat, out, attended):
     block = pl.program_id(0)
     size = ids.shape[0]
     emb = normalized(where_sum[...] + pick(hot_token(ids[...]), [t1[...], t2[...], t3[...]]))
-    queries = jnp.dot(emb, w_query[...], precision=HIGHEST) * HD ** (-0.5)
+    e = parts_of(emb)
+    w = parts_of(w_query[...])
+    near_w = jnp.concatenate([w[0], w[1]], axis=1)
+    wide = jnp.dot(e[0], near_w, preferred_element_type=jnp.float32)
+    wide = wide + jnp.dot(e[1], near_w, preferred_element_type=jnp.float32)
+    wide = wide[:, :128] + wide[:, 128:]
+    wide = wide + jnp.dot(
+        jnp.concatenate([e[0], e[2]], axis=1),
+        jnp.concatenate([w[2], w[0]], axis=0),
+        preferred_element_type=jnp.float32,
+    )
+    queries = wide * HD ** (-0.5)
     q = [part.astype(jnp.float32) for part in parts_of(queries)]
     low = low_lanes(size)
     where = index[0] * POS_DEV + lax.broadcasted_iota(jnp.int32, (size, POS_DEV), 1)
@@ -163,7 +173,22 @@
     out[pl.ds(8, chunks, stride=9), :] = jnp.sum(jnp.where((lane & 7) == lat, level, 0.0), axis=1)
 
 
-def project_kernel(states, weights, out):
+def prepare_kernel(weights, out_cat, in_cat, down_cat):
+    for c in range(8):
+        rows = pl.ds(c * 128, 128)
+        near, rest, _ = parts_of(weights[:, c * 32 : c * 32 + 16, :].reshape(128, 128))
+        out_cat[rows, 0:128] = near
+        out_cat[rows, 128:256] = rest
+        near, rest, _ = parts_of(weights[:, c * 32 + 16 : c * 32 + 32, :].reshape(128, 128))
+        near, rest = near.astype(jnp.float32), rest.astype(jnp.float32)
+        low = low_lanes(128)
+        in_cat[rows, :] = pair(low, near, rest, 0).astype(jnp.bfloat16)
+        down = pair(low, near, rest, 1)
+        down_cat[rows, 0:128] = down.astype(jnp.bfloat16)
+        down_cat[rows, 128:256] = down.astype(jnp.bfloat16)
+
+
+def project_kernel(states, out_cat, out):
     levels = states[pl.ds(8, 64, stride=9), :]
     low = low_lanes(64)
     rows = []
@@ -172,34 +197,30 @@
         share = jnp.exp(level - jnp.max(level, axis=0, keepdims=True))
         value = jnp.sum(share * states[pl.ds(r, 64, stride=9), :], axis=0, keepdims=True)
         rows.append(value / jnp.sum(share, axis=0, keepdims=True))
-    attended = jnp.concatenate(rows, axis=0)
+    near, rest, _ = parts_of(jnp.concatenate(rows, axis=0))
+    near, rest = near.astype(jnp.float32), rest.astype(jnp.float32)
+    left = jnp.concatenate(
+        [jnp.concatenate([near, near], axis=1), jnp.concatenate([rest, rest], axis=1)], axis=0
+    ).astype(jnp.bfloat16)
+    both = lax.dot_general(left, out_cat[...], NT, preferred_element_type=jnp.float32)
+    partial = both[0:8] + both[8:16]
     for c in range(8):
-        block = weights[:, c * 32 : c * 32 + 16, :].reshape(128, 128)
-        out[pl.ds(c, 8, stride=8), :] = lax.dot_general(
-            attended, block, NT, precision=HIGHEST, preferred_element_type=jnp.float32
-        )
-
-
-def latent_kernel(rows, weights, out):
-    pieces = [rows[pl.ds(c, 64, stride=8), :] for c in range(8)]
-    mean = sum(jnp.sum(p, axis=-1, keepdims=True) for p in pieces) * (1.0 / D)
-    pieces = [p - mean for p in pieces]
-    spread = sum(jnp.sum(p * p, axis=-1, keepdims=True) for p in pieces) * (1.0 / D)
-    scale = lax.rsqrt(spread + 1e-05)
-    hidden = None
-    blocks = []
+        out[pl.ds(c, 8, stride=8), :] = partial[:, c * 128 : (c + 1) * 128]
+
+
+def latent_kernel(rows, in_cat, down_cat, out):
+    row = jnp.concatenate([rows[pl.ds(c, 64, stride=8), :] for c in range(8)], axis=1)
+    near, rest, _ = parts_of(normalized(row))
+    raw = jnp.dot(
+        jnp.concatenate([near, rest], axis=0), in_cat[...], preferred_element_type=jnp.float32
+    )
+    raw = raw[0:64] + raw[64:128]
+    hidden = jax.nn.gelu(raw + pltpu.roll(raw, HD, 1))
+    near, rest, _ = parts_of(hidden)
+    left = jnp.concatenate([near, rest], axis=1)
+    down = lax.dot_general(left, down_cat[...], NT, preferred_element_type=jnp.float32)
     for c in range(8):
-        block = weights[:, c * 32 + 16 : c * 32 + 32, :].reshape(128, 128)
-        blocks.append(block)
-        part = jnp.dot(pieces[c] * scale, block, precision=HIGHEST)
-        hidden = part if hidden is None else hidden + part
-    hidden = jax.nn.gelu(pltpu.roll(hidden, 64, 1))
-    lane = lax.broadcasted_iota(jnp.int32, hidden.shape, 1)
-    hidden = jnp.where(lane >= 64, hidden, 0.0)
-    for c in range(8):
-        out[pl.ds(c, 64, stride=8), :] = lax.dot_general(
-            hidden, blocks[c], NT, precision=HIGHEST, preferred_element_type=jnp.float32
-        )
+        out[pl.ds(c, 64, stride=8), :] = down[:, c * 128 : (c + 1) * 128]
 
 
 VMEM = pl.BlockSpec(memory_space=pltpu.VMEM)
@@ -220,6 +241,12 @@
 
 def per_device(token_ids, token_table, row_table, col_table, chan_table, w_query, w_key, w_value, w_out, w_in, w_down):
     index = lax.axis_index(POS).astype(jnp.int32).reshape(1)
+
+    bf16 = lambda *dims: jax.ShapeDtypeStruct(dims, jnp.bfloat16)
+    whole = lambda *dims: pl.BlockSpec(dims, lambda i: (0,) * len(dims))
+    slab = lambda *dims: pl.BlockSpec(dims, lambda i: (i,) + (0,) * (len(dims) - 1))
+    lanes = lambda *dims: pl.BlockSpec(dims, lambda i: (0, i))
+    middle = lambda *dims: pl.BlockSpec(dims, lambda i: (0, i, 0))
 
     with jax.named_scope("weights"):
         own_ids = token_ids[POS_DEV - LAT :].astype(jnp.float32).reshape(4, 128)
@@ -235,32 +262,43 @@
             axis=1,
         )
         packed = exchange(packed, "z")
+
+    width = 256
+    tables = pl.pallas_call(
+        tables_kernel,
+        grid=(D // width,),
+        in_specs=[lanes(VOCAB, width), lanes(ROWS_USED, width), lanes(IMG, width), lanes(3, width)],
+        out_specs=[lanes(VOCAB, width)] * 3 + [lanes(384, width)] * 3 + [lanes(LAT, width)],
+        out_shape=[bf16(VOCAB, D)] * 3 + [bf16(384, D)] * 3 + [shape(LAT, D)],
+        compiler_params=params(),
+        cost_estimate=pl.CostEstimate(flops=2 * 10**9, transcendentals=0, bytes_accessed=8 * 10**6),
+        name="tables",
+    )(token_table, row_table, col_table, chan_table)
+    packed, tables = lax.optimization_barrier((packed, tables))
+    *splits, where_sum = tables
+    tokens = splits[:3]
+
+    with jax.named_scope("columns"):
         packed = jnp.concatenate([packed[:, :32, :].reshape(256, 128), packed[7, 32:, :]], axis=0)
         weights = exchange(jnp.broadcast_to(packed[None], (8, 264, 128)), COLUMN)
         latent_ids = weights[7, 256:260, :].astype(jnp.int32).reshape(LAT, 1)
 
-    steps = 4
-    block, size = POS_DEV // steps, LAT // steps
-    bf16 = lambda *dims: jax.ShapeDtypeStruct(dims, jnp.bfloat16)
-    whole = lambda *dims: pl.BlockSpec(dims, lambda i: (0,) * len(dims))
-    slab = lambda *dims: pl.BlockSpec(dims, lambda i: (i,) + (0,) * (len(dims) - 1))
-    middle = lambda *dims: pl.BlockSpec(dims, lambda i: (0, i, 0))
-    key_cat, value_cat, where_sum, *tokens = pl.pallas_call(
+    block = POS_DEV // KEY_STEPS
+    key_cat, value_cat = pl.pallas_call(
         keys_kernel,
-        grid=(steps,),
-        in_specs=[SMEM, slab(block, 1), whole(VOCAB, D), whole(IMG, D), whole(IMG, D), whole(3, D)]
-        + [whole(D, 128)] * 2,
-        out_specs=[middle(2, block, 512), middle(2, block, 256), slab(size, D)] + [whole(VOCAB, D)] * 3,
-        out_shape=[bf16(2, POS_DEV, 512), bf16(2, POS_DEV, 256), shape(LAT, D)] + [bf16(VOCAB, D)] * 3,
-        scratch_shapes=[pltpu.VMEM((384, D), jnp.bfloat16)] * 3,
+        grid=(KEY_STEPS,),
+        in_specs=[SMEM, slab(block, 1)] + [whole(VOCAB, D)] * 3 + [whole(384, D)] * 3 + [whole(D, 128)] * 2,
+        out_specs=[middle(2, block, 512), middle(2, block, 256)],
+        out_shape=[bf16(2, POS_DEV, 512), bf16(2, POS_DEV, 256)],
         compiler_params=params(),
         cost_estimate=pl.CostEstimate(flops=8 * 10**9, transcendentals=0, bytes_accessed=10**7),
         name="keys",
-    )(index, token_ids.reshape(POS_DEV, 1), token_table, row_table, col_table, chan_table, w_key, w_value)
-
+    )(index, token_ids.reshape(POS_DEV, 1), *splits, w_key, w_value)
+
+    size = LAT // LATENT_STEPS
     states = pl.pallas_call(
         attend_kernel,
-        grid=(steps,),
+        grid=(LATENT_STEPS,),
         in_specs=[SMEM, slab(size, 1), slab(size, D)]
         + [whole(VOCAB, D)] * 3
         + [whole(D, 128), whole(2, POS_DEV, 512), whole(2, POS_DEV, 256)],
@@ -274,6 +312,15 @@
 
     with jax.named_scope("states"):
         states = exchange(states.reshape(64, 1, 1152), POS).reshape(64 * 9, 128)
+    out_cat, in_cat, down_cat = pl.pallas_call(
+        prepare_kernel,
+        in_specs=[VMEM],
+        out_specs=[VMEM] * 3,
+        out_shape=[bf16(D, 256), bf16(D, 128), bf16(D, 256)],
+        compiler_params=params(),
+        cost_estimate=pl.CostEstimate(flops=10**9, transcendentals=0, bytes_accessed=3 * 10**6),
+        name="prepare",
+    )(weights)
     partial_rows = pl.pallas_call(
         project_kernel,
         in_specs=[VMEM, VMEM],
@@ -281,18 +328,18 @@
         out_shape=shape(64, 128),
         compiler_params=params(),
         name="project",
-    )(states, weights)
+    )(states, out_cat)
     with jax.named_scope("projected"):
         projected = jnp.sum(exchange(partial_rows.reshape(8, 8, 128), HEAD), axis=0)
         rows = exchange(jnp.broadcast_to(projected[None], (64, 8, 128)), SHARERS)
     outs = pl.pallas_call(
         latent_kernel,
-        in_specs=[VMEM, VMEM],
+        in_specs=[VMEM] * 3,
         out_specs=VMEM,
         out_shape=shape(512, 128),
         compiler_params=params(),
         name="latent",
-    )(rows.reshape(512, 128), weights)
+    )(rows.reshape(512, 128), in_cat, down_cat)
     with jax.named_scope("result"):
         own = projected + jnp.sum(exchange(outs.reshape(64, 8, 128), SHARERS), axis=0)
         return exchange(jnp.broadcast_to(own[None], (8, 8, 128)), HEAD).reshape(8, D)

time: 161 us -> 157 us (0.975)
  blocking collectives: 106 us -> 67.8 us
  starting transfers between devices: 5.16 us -> 25 us
  waiting for transfers between devices: 0.01 us -> 11.4 us
    all_to_all x6 -> x4, blocking collectives: 106 us -> 67.8 us  [exchange(): return lax.all_to_all(value, axes, 0, 0)]
    all_to_all x1 -> x3, starting transfers between devices: 5.16 us -> 25 us  [exchange(): return lax.all_to_all(value, axes, 0, 0)]
    all_to_all x1 -> x3, waiting for transfers between devices: 0.01 us -> 11.4 us  [exchange(): return lax.all_to_all(value, axes, 0, 0)]
    pallas_call x3 -> x5, Pallas kernels: 39.6 us -> 41.1 us  [the longest x1 19.4 us: per_device(): pl.pallas_call(keys_kernel, grid=(KEY_STEPS,), in_specs=[SMEM, slab(block...]
  transfers between devices with their start and end apart: 1 -> 3, of which waited for: 0 -> 2; matrix products, arithmetic and copies ran while one was open for 1% -> 1% of each run, Pallas kernels for 12% -> 18%
where the time goes in v3:
time: 157 us; the launch traced here: 156 us
  blocking collectives  67.8 us (43%)
  Pallas kernels  43.3 us (28%)
  starting transfers between devices  25 us (16%)
  waiting for transfers between devices  11.4 us (7%)
  local copies, waits for them, and re-layouts  6.93 us (4%)
    all_to_all x4, blocking collectives, exchange(): return lax.all_to_all(value, axes, 0, 0)  67.8 us
    all_to_all x3, starting transfers between devices, exchange(): return lax.all_to_all(value, axes, 0, 0)  25 us
    pallas_call x1, Pallas kernels, per_device(): pl.pallas_call(keys_kernel, grid=(KEY_STEPS,), in_specs=[SMEM, slab(block...  19.4 us
    all_to_all x3, waiting for transfers between devices, exchange(): return lax.all_to_all(value, axes, 0, 0)  11.4 us
    pallas_call x1, Pallas kernels, per_device(): pl.pallas_call(attend_kernel, grid=(LATENT_STEPS,), in_specs=[SMEM, slab(...  10.8 us
    pallas_call x1, Pallas kernels, per_device(): pl.pallas_call(tables_kernel, grid=(D // width,), in_specs=[lanes(VOCAB,...  5.75 us
  transfers between devices with their start and end apart: 3, of which 2 were waited for; matrix products, arithmetic and copies ran while one was open for 1% of the time, Pallas kernels for 18%

profile of v3, /device:TPU:1, one launch (start us, length us, event | category | flops | bytes accessed | tf_op | source)
XLA Modules:
  0.0 156.0 jit_solution(14818871711964972000)
XLA Ops:
  0.0 0.8 reshape.66
  0.9 0.8 reshape.65
  1.7 0.7 convert_bitcast_fusion
  2.4 0.7 broadcast_in_dim.10
  3.1 0.8 pad_maximum_fusion
  3.9 10.9 %all-to-all-start = ((f32[8,40,128]{2,1,0:T(8,128)}), f32[8,40,128]{2,1,0:T(8,128)S(1)}, u32[]{:S(2)}, u32[]{:S(2)}) async-start(f32[8,40,128]{2,1,0:T(8,128)} %pad_maximum_fusion), calls=%async_computation | async-start | bytes 327680 | tf_op jit(solution)/shard_map/weights/all_to_all | solution.py:239
  14.7 5.7 %tables.1 = (bf16[256,1024]{1,0:T(8,128)(2,1)}, bf16[256,1024]{1,0:T(8,128)(2,1)}, bf16[256,1024]{1,0:T(8,128)(2,1)}, bf16[384,1024]{1,0:T(8,128)(2,1)}, bf16[38...) custom-call(f32[256,1024]{1,0:T(8,128)} %token_.1, f32[256,1024]{1,0:T(8,128)} %row.1, ...), custom_call_target="tpu_custom_call" | custom-call | flops 2000000000 | bytes 8000000 | tf_op jit(solution)/shard_map/tables/pallas_call | solution.py:267
  20.5 2.5 %all-to-all-done = f32[8,40,128]{2,1,0:T(8,128)S(1)} async-done(((f32[8,40,128]{2,1,0:T(8,128)}), f32[8,40,128]{2,1,0:T(8,128)S(1)}, u32[]{:S(2)}, u32[]{:S(2)}) %all-to-all-start) | async-done | bytes 163872 | tf_op jit(solution)/shard_map/weights/all_to_all | solution.py:239
  23.0 1.0 broadcast_in_dim.12
  24.0 0.0 copy-start.2
  24.0 5.2 %all-to-all-start.1 = ((f32[8,264,128]{2,1,0:T(8,128)}), f32[8,264,128]{2,1,0:T(8,128)S(1)}, u32[]{:S(2)}, u32[]{:S(2)}) async-start(f32[8,264,128]{2,1,0:T(8,128)} %broadcast_in_dim.12), calls=%async_computation.1 | async-start | bytes 2162688 | tf_op jit(solution)/shard_map/columns/all_to_all | solution.py:239
  29.2 0.0 copy-done.2
  29.2 1.1 copy.21.ids
  30.3 19.4 %keys.1 = (bf16[2,1024,512]{2,1,0:T(8,128)(2,1)}, bf16[2,1024,256]{2,1,0:T(8,128)(2,1)}) custom-call(s32[1]{0:T(128)} %bitcast.index, s32[1024,1]{1,0:T(8,128)} %copy.21.ids, bf16[256,1024]{1,0:T(8,128)(2,1)} %get-tuple-element.34.t1, bf16[256,1024]{1,0:T(8,128)(2,1)} %get-tuple-element.35.t2, bf16[256,1024]{1,0:T(8,128)(2,1)} %get-tuple-element.36.t3, ...), custom_call_target="tpu_custom_call" | custom-call | flops 8000000000 | bytes 10000000 | tf_op jit(solution)/shard_map/keys/pallas_call | solution.py:287
  49.7 0.0 all-to-all-done.1.weights
  49.7 0.0 copy-start.1
  49.7 1.0 copy.22.ids
  50.7 10.8 %attend.1 = f32[576,128]{1,0:T(8,128)} custom-call(s32[1]{0:T(128)} %bitcast.index, s32[512,1]{1,0:T(8,128)} %copy.22.ids, f32[512,1024]{1,0:T(8,128)} %get-tuple-element.33.where_sum, bf16[256,1024]{1,0:T(8,128)(2,1)} %get-tuple-element.34.t1, bf16[256,1024]{1,0:T(8,128)(2,1)} %get-tuple-element.35.t2, bf16[256,1024]{1,0:T(8,128)(2,1)} %get-tuple-element.36.t3, ...), custom_call_target="tpu_custom_call" | custom-call | flops 6000000000 | bytes 10000000 | tf_op jit(solution)/shard_map/attend/pallas_call | solution.py:299
  61.6 0.0 copy-done.1
  61.6 9.0 %all-to-all-start.2 = ((f32[64,1,1152]{2,1,0:T(1,128)}), f32[64,1,1152]{2,1,0:T(1,128)S(1)}, u32[]{:S(2)}, u32[]{:S(2)}) async-start(f32[64,1,1152]{2,1,0:T(1,128)} %bitcast.30), calls=%async_computation.2 | async-start | bytes 589824 | tf_op jit(solution)/shard_map/states/all_to_all | solution.py:239
  70.5 2.5 %prepare.1 = (bf16[1024,256]{1,0:T(8,128)(2,1)}, bf16[1024,128]{1,0:T(8,128)(2,1)}, bf16[1024,256]{1,0:T(8,128)(2,1)}) custom-call(f32[8,264,128]{2,1,0:T(8,128)} %copy-done.1), custom_call_target="tpu_custom_call" | custom-call | flops 1000000000 | bytes 3000000 | tf_op jit(solution)/shard_map/prepare/pallas_call | solution.py:315
  73.1 8.9 %all-to-all-done.2 = f32[64,1,1152]{2,1,0:T(1,128)S(1)} async-done(((f32[64,1,1152]{2,1,0:T(1,128)}), f32[64,1,1152]{2,1,0:T(1,128)S(1)}, u32[]{:S(2)}, u32[]{:S(2)}) %all-to-all-start.2) | async-done | bytes 294944 | tf_op jit(solution)/shard_map/states/all_to_all | solution.py:239
  81.9 0.0 copy-start
  81.9 0.7 copy-done
  82.7 2.2 %project.1 = f32[64,128]{1,0:T(8,128)} custom-call(f32[576,128]{1,0:T(8,128)} %bitcast.26, bf16[1024,256]{1,0:T(8,128)(2,1)} %get-tuple-element.42.out_cat), custom_call_target="tpu_custom_call" | custom-call | tf_op jit(solution)/shard_map/project/pallas_call | solution.py:324
  84.9 16.7 %all_to_all.35 = f32[8,8,128]{2,1,0:T(8,128)S(1)} all-to-all(f32[8,8,128]{2,1,0:T(8,128)} %bitcast.34), channel_id=1, replica_groups=mesh['z'=8,'ylo'=2,'x'=4,'yhi'=4,'core'=2] {'yhi','core'}, dimensions={0} | all-to-all | bytes 65536 | tf_op jit(solution)/shard_map/projected/all_to_all | solution.py:239
  101.6 20.5 %all_to_all.36 = f32[64,8,128]{2,1,0:T(8,128)} all-to-all(f32[64,8,128]{2,1,0:T(8,128)S(1)} %broadcast_in_dim.13), channel_id=1, replica_groups=mesh['z'=8,'ylo'=2,'x'=4,'yhi'=4,'core'=2] {'z','yhi','core'}, dimensions={0} | all-to-all | bytes 524288 | tf_op jit(solution)/shard_map/projected/all_to_all | solution.py:239
  122.2 2.6 %latent.1 = f32[512,128]{1,0:T(8,128)} custom-call(f32[512,128]{1,0:T(8,128)} %bitcast.27, bf16[1024,128]{1,0:T(8,128)(2,1)} %get-tuple-element.43.in_cat, bf16[1024,256]{1,0:T(8,128)(2,1)} %get-tuple-element.44.down_cat), custom_call_target="tpu_custom_call" | custom-call | tf_op jit(solution)/shard_map/latent/pallas_call | solution.py:335
  124.8 20.2 %all_to_all.37 = f32[64,8,128]{2,1,0:T(8,128)S(1)} all-to-all(f32[64,8,128]{2,1,0:T(8,128)} %bitcast.28), channel_id=1, replica_groups=mesh['z'=8,'ylo'=2,'x'=4,'yhi'=4,'core'=2] {'z','yhi','core'}, dimensions={0} | all-to-all | bytes 524288 | tf_op jit(solution)/shard_map/result/all_to_all | solution.py:239
  144.9 0.1 reduce_sum.19
  145.0 10.4 %all_to_all.38 = f32[8,8,128]{2,1,0:T(8,128)S(1)} all-to-all(f32[8,8,128]{2,1,0:T(8,128)S(1)} %broadcast_in_dim.14), channel_id=1, replica_groups=mesh['z'=8,'ylo'=2,'x'=4,'yhi'=4,'core'=2] {'yhi','core'}, dimensions={0} | all-to-all | bytes 65536 | tf_op jit(solution)/shard_map/result/all_to_all | solution.py:239
  155.4 0.6 copy.30
  (12 shorter events, 0.1 us)
Async XLA Ops:
  3.9 19.1 %all-to-all-start = ((f32[8,40,128]{2,1,0:T(8,128)}), f32[8,40,128]{2,1,0:T(8,128)S(1)}, u32[]{:S(2)}, u32[]{:S(2)}) async-start(f32[8,40,128]{2,1,0:T(8,128)} %pad_maximum_fusion), calls=%async_computation | async-start | bytes 327680 | tf_op jit(solution)/shard_map/weights/all_to_all | solution.py:239
  24.0 5.2 %copy-start.2 = (s32[1024]{0:T(1024)S(1)}, s32[1024]{0:T(1024)}, u32[]{:S(2)}) copy-start(s32[1024]{0:T(1024)} %param.11) | copy-start | bytes 12292
  24.0 25.6 %all-to-all-start.1 = ((f32[8,264,128]{2,1,0:T(8,128)}), f32[8,264,128]{2,1,0:T(8,128)S(1)}, u32[]{:S(2)}, u32[]{:S(2)}) async-start(f32[8,264,128]{2,1,0:T(8,128)} %broadcast_in_dim.12), calls=%async_computation.1 | async-start | bytes 2162688 | tf_op jit(solution)/shard_map/columns/all_to_all | solution.py:239
  49.7 11.9 %copy-start.1 = (f32[8,264,128]{2,1,0:T(8,128)}, f32[8,264,128]{2,1,0:T(8,128)S(1)}, u32[]{:S(2)}) copy-start(f32[8,264,128]{2,1,0:T(8,128)S(1)} %all-to-all-done.1.weights) | copy-start | bytes 3244036
  61.6 20.4 %all-to-all-start.2 = ((f32[64,1,1152]{2,1,0:T(1,128)}), f32[64,1,1152]{2,1,0:T(1,128)S(1)}, u32[]{:S(2)}, u32[]{:S(2)}) async-start(f32[64,1,1152]{2,1,0:T(1,128)} %bitcast.30), calls=%async_computation.2 | async-start | bytes 589824 | tf_op jit(solution)/shard_map/states/all_to_all | solution.py:239
  81.9 0.7 copy-start

commit v4 on v3

--- a/solution.py
+++ b/solution.py
@@ -14,8 +14,10 @@
 POSITIONS = 65536
 VOCAB = 256
 ROWS_USED = 88
-KEY_STEPS = 2
-LATENT_STEPS = 2
+KEY_STEPS = 1
+LATENT_STEPS = 1
+KEY_PARTS = 2
+QUERY_PARTS = 4
 
 POS = ("z", "ylo", "x")
 HEAD = ("yhi", "core")
@@ -60,6 +62,17 @@
     return jnp.concatenate([hot(lane == (pixel & 255)), hot(in_tail)], axis=1)
 
 
+def id_columns(ids, size, skip):
+    turned = jnp.transpose(ids)
+    column = lax.broadcasted_iota(jnp.int32, turned.shape, 1)
+    start = skip + pl.program_id(0) * (size // 128)
+    picked = [
+        jnp.sum(jnp.where(column == start + i, turned, 0.0), axis=1, keepdims=True)
+        for i in range(size // 128)
+    ]
+    return jnp.concatenate(picked, axis=0).astype(jnp.int32)
+
+
 def hot_token(ids):
     return hot(lax.broadcasted_iota(jnp.int32, (ids.shape[0], VOCAB), 1) == ids)
 
@@ -86,6 +99,16 @@
     if head == 0:
         return jnp.where(low, first, pltpu.roll(second, HD, 1))
     return jnp.where(low, pltpu.roll(first, HD, 1), second)
+
+
+def pack_kernel(ids, w_out, w_in, w_down, packed):
+    low = low_lanes(16)
+    own_ids = ids[...].astype(jnp.float32)
+    for b in range(8):
+        lanes = slice(b // 2 * 128, b // 2 * 128 + 128)
+        packed[b, 0:16, :] = w_out[...]
+        packed[b, 16:32, :] = pair(low, w_in[:, lanes], w_down[:, lanes], b % 2)
+        packed[b, 32:40, :] = own_ids
 
 
 def tables_kernel(token, row, col, chan, t1, t2, t3, p1, p2, p3, where_sum):
@@ -99,12 +122,19 @@
 
 
 def keys_kernel(index, ids, t1, t2, t3, p1, p2, p3, w_key, w_value, key_cat, value_cat):
-    size = ids.shape[0]
+    size = POS_DEV // KEY_STEPS
+    part_size = size // KEY_PARTS
     first = index[0] * POS_DEV + pl.program_id(0) * size
-    total = pick(hot_place(first, size), [p1[...], p2[...], p3[...]])
-    total = total + pick(hot_token(ids[...]), [t1[...], t2[...], t3[...]])
-    emb = normalized(total)
-    both = jnp.dot(emb, jnp.concatenate([w_key[...], w_value[...]], axis=1), precision=HIGHEST)
+    columns = id_columns(ids[...].astype(jnp.float32), size, 0)
+    places = [p1[...], p2[...], p3[...]]
+    tokens = [t1[...], t2[...], t3[...]]
+    embs = []
+    for i in range(KEY_PARTS):
+        total = pick(hot_place(first + i * part_size, part_size), places)
+        total = total + pick(hot_token(columns[i * part_size : (i + 1) * part_size]), tokens)
+        embs.append(normalized(total))
+    wide = jnp.concatenate([w_key[...], w_value[...]], axis=1)
+    both = jnp.concatenate([jnp.dot(emb, wide, precision=HIGHEST) for emb in embs], axis=0)
     keys, values = both[:, :128], both[:, 128:]
     low = low_lanes(size)
     k = [part.astype(jnp.float32) for part in parts_of(keys)]
@@ -122,20 +152,27 @@
 
 def attend_kernel(index, ids, where_sum, t1, t2, t3, w_query, key_cat, value_cat, out, attended):
     block = pl.program_id(0)
-    size = ids.shape[0]
-    emb = normalized(where_sum[...] + pick(hot_token(ids[...]), [t1[...], t2[...], t3[...]]))
-    e = parts_of(emb)
+    size = where_sum.shape[0]
+    columns = id_columns(ids[...], size, (POS_DEV - LAT) // 128)
+    tokens = [t1[...], t2[...], t3[...]]
     w = parts_of(w_query[...])
     near_w = jnp.concatenate([w[0], w[1]], axis=1)
-    wide = jnp.dot(e[0], near_w, preferred_element_type=jnp.float32)
-    wide = wide + jnp.dot(e[1], near_w, preferred_element_type=jnp.float32)
-    wide = wide[:, :128] + wide[:, 128:]
-    wide = wide + jnp.dot(
-        jnp.concatenate([e[0], e[2]], axis=1),
-        jnp.concatenate([w[2], w[0]], axis=0),
-        preferred_element_type=jnp.float32,
-    )
-    queries = wide * HD ** (-0.5)
+    far_w = jnp.concatenate([w[2], w[0]], axis=0)
+    part_size = size // QUERY_PARTS
+    queries = []
+    for i in range(QUERY_PARTS):
+        rows = slice(i * part_size, (i + 1) * part_size)
+        e = parts_of(normalized(where_sum[rows] + pick(hot_token(columns[rows]), tokens)))
+        wide = jnp.dot(e[0], near_w, preferred_element_type=jnp.float32)
+        wide = wide + jnp.dot(e[1], near_w, preferred_element_type=jnp.float32)
+        wide = wide[:, :128] + wide[:, 128:]
+        queries.append(
+            wide
+            + jnp.dot(
+                jnp.concatenate([e[0], e[2]], axis=1), far_w, preferred_element_type=jnp.float32
+            )
+        )
+    queries = jnp.concatenate(queries, axis=0) * HD ** (-0.5)
     q = [part.astype(jnp.float32) for part in parts_of(queries)]
     low = low_lanes(size)
     where = index[0] * POS_DEV + lax.broadcasted_iota(jnp.int32, (size, POS_DEV), 1)
@@ -249,18 +286,14 @@
     middle = lambda *dims: pl.BlockSpec(dims, lambda i: (0, i, 0))
 
     with jax.named_scope("weights"):
-        own_ids = token_ids[POS_DEV - LAT :].astype(jnp.float32).reshape(4, 128)
-        own_ids = jnp.concatenate([own_ids, jnp.zeros((4, 128), jnp.float32)], axis=0)
-        own_in = w_in.reshape(16, 8, 64).transpose(1, 0, 2)
-        own_down = w_down.reshape(8, 64, 16).transpose(0, 2, 1)
-        packed = jnp.concatenate(
-            [
-                jnp.broadcast_to(w_out.T[None], (8, 16, 128)),
-                jnp.concatenate([own_in, own_down], axis=2),
-                jnp.broadcast_to(own_ids[None], (8, 8, 128)),
-            ],
-            axis=1,
-        )
+        packed = pl.pallas_call(
+            pack_kernel,
+            in_specs=[VMEM] * 4,
+            out_specs=VMEM,
+            out_shape=shape(8, 40, 128),
+            compiler_params=params(),
+            name="pack",
+        )(token_ids.reshape(8, 128), w_out.T, w_in, w_down.T)
         packed = exchange(packed, "z")
 
     width = 256
@@ -281,25 +314,24 @@
     with jax.named_scope("columns"):
         packed = jnp.concatenate([packed[:, :32, :].reshape(256, 128), packed[7, 32:, :]], axis=0)
         weights = exchange(jnp.broadcast_to(packed[None], (8, 264, 128)), COLUMN)
-        latent_ids = weights[7, 256:260, :].astype(jnp.int32).reshape(LAT, 1)
 
     block = POS_DEV // KEY_STEPS
     key_cat, value_cat = pl.pallas_call(
         keys_kernel,
         grid=(KEY_STEPS,),
-        in_specs=[SMEM, slab(block, 1)] + [whole(VOCAB, D)] * 3 + [whole(384, D)] * 3 + [whole(D, 128)] * 2,
+        in_specs=[SMEM, whole(8, 128)] + [whole(VOCAB, D)] * 3 + [whole(384, D)] * 3 + [whole(D, 128)] * 2,
         out_specs=[middle(2, block, 512), middle(2, block, 256)],
         out_shape=[bf16(2, POS_DEV, 512), bf16(2, POS_DEV, 256)],
         compiler_params=params(),
         cost_estimate=pl.CostEstimate(flops=8 * 10**9, transcendentals=0, bytes_accessed=10**7),
         name="keys",
-    )(index, token_ids.reshape(POS_DEV, 1), *splits, w_key, w_value)
+    )(index, token_ids.reshape(8, 128), *splits, w_key, w_value)
 
     size = LAT // LATENT_STEPS
     states = pl.pallas_call(
         attend_kernel,
         grid=(LATENT_STEPS,),
-        in_specs=[SMEM, slab(size, 1), slab(size, D)]
+        in_specs=[SMEM, whole(8, 128), slab(size, D)]
         + [whole(VOCAB, D)] * 3
         + [whole(D, 128), whole(2, POS_DEV, 512), whole(2, POS_DEV, 256)],
         out_specs=slab(size // 8 * 9, 128),
@@ -308,7 +340,7 @@
         compiler_params=params(),
         cost_estimate=pl.CostEstimate(flops=6 * 10**9, transcendentals=10**6, bytes_accessed=10**7),
         name="attend",
-    )(index, latent_ids, where_sum, *tokens, w_query, key_cat, value_cat)
+    )(index, weights[7, 256:264, :], where_sum, *tokens, w_query, key_cat, value_cat)
 
     with jax.named_scope("states"):
         states = exchange(states.reshape(64, 1, 1152), POS).reshape(64 * 9, 128)

time: 157 us -> 148 us (0.943)
  local copies, waits for them, and re-layouts: 6.93 us -> 3.05 us
  Pallas kernels: 43.3 us -> 39.6 us
    pallas_call x2 -> x3, Pallas kernels: 30.2 us -> 26.6 us  [the longest x1 13.8 us: per_device(): pl.pallas_call(keys_kernel, grid=(KEY_STEPS,), in_specs=[SMEM, whole(8, 1...]
    reshape x5 -> x0, local copies, waits for them, and re-layouts: 2.75 us -> none  [the longest x1 1.05 us: per_device(): token_ids.reshape(POS_DEV, 1)]
  transfers between devices with their start and end apart: 3 -> 3, of which waited for: 2 -> 2; matrix products, arithmetic and copies ran while one was open for 1% -> 0% of each run, Pallas kernels for 18% -> 15%
where the time goes in v4:
time: 148 us; the launch traced here: 147 us
  blocking collectives  67.8 us (46%)
  Pallas kernels  39.6 us (27%)
  starting transfers between devices  24.7 us (17%)
  waiting for transfers between devices  11.5 us (8%)
  local copies, waits for them, and re-layouts  3.05 us (2%)
    all_to_all x4, blocking collectives, exchange(): return lax.all_to_all(value, axes, 0, 0)  67.8 us
    all_to_all x3, starting transfers between devices, exchange(): return lax.all_to_all(value, axes, 0, 0)  24.7 us
    pallas_call x1, Pallas kernels, per_device(): pl.pallas_call(keys_kernel, grid=(KEY_STEPS,), in_specs=[SMEM, whole(8, 1...  13.8 us
    all_to_all x3, waiting for transfers between devices, exchange(): return lax.all_to_all(value, axes, 0, 0)  11.5 us
    pallas_call x1, Pallas kernels, per_device(): pl.pallas_call(attend_kernel, grid=(LATENT_STEPS,), in_specs=[SMEM, whole...  11.2 us
    pallas_call x1, Pallas kernels, per_device(): pl.pallas_call(tables_kernel, grid=(D // width,), in_specs=[lanes(VOCAB,...  5.77 us
  transfers between devices with their start and end apart: 3, of which 2 were waited for; matrix products, arithmetic and copies ran while one was open for 0% of the time, Pallas kernels for 15%

profile of v4, /device:TPU:1, one launch (start us, length us, event | category | flops | bytes accessed | tf_op | source)
XLA Modules:
  0.0 146.9 jit_solution(483249273317309575)
XLA Ops:
  0.0 1.6 %pack.1 = f32[8,40,128]{2,1,0:T(8,128)} custom-call(s32[8,128]{1,0:T(8,128)} %bitcast.27, f32[16,128]{1,0:T(8,128)} %bitcast.26, f32[16,512]{1,0:T(8,128)} %w_in.1, f32[16,512]{1,0:T(8,128)} %bitcast.25), custom_call_target="tpu_custom_call" | custom-call | tf_op jit(solution)/shard_map/weights/pack/pallas_call | solution.py:289
  1.6 10.9 %all-to-all-start = ((f32[8,40,128]{2,1,0:T(8,128)}), f32[8,40,128]{2,1,0:T(8,128)S(1)}, u32[]{:S(2)}, u32[]{:S(2)}) async-start(f32[8,40,128]{2,1,0:T(8,128)} %pack.1), calls=%async_computation | async-start | bytes 327680 | tf_op jit(solution)/shard_map/weights/all_to_all | solution.py:276
  12.4 5.8 %tables.1 = (bf16[256,1024]{1,0:T(8,128)(2,1)}, bf16[256,1024]{1,0:T(8,128)(2,1)}, bf16[256,1024]{1,0:T(8,128)(2,1)}, bf16[384,1024]{1,0:T(8,128)(2,1)}, bf16[38...) custom-call(f32[256,1024]{1,0:T(8,128)} %token_.1, f32[256,1024]{1,0:T(8,128)} %row.1, ...), custom_call_target="tpu_custom_call" | custom-call | flops 2000000000 | bytes 8000000 | tf_op jit(solution)/shard_map/tables/pallas_call | solution.py:300
  18.2 2.4 %all-to-all-done = f32[8,40,128]{2,1,0:T(8,128)S(1)} async-done(((f32[8,40,128]{2,1,0:T(8,128)}), f32[8,40,128]{2,1,0:T(8,128)S(1)}, u32[]{:S(2)}, u32[]{:S(2)}) %all-to-all-start) | async-done | bytes 163872 | tf_op jit(solution)/shard_map/weights/all_to_all | solution.py:276
  20.7 1.0 broadcast_in_dim.6
  21.7 5.0 %all-to-all-start.1 = ((f32[8,264,128]{2,1,0:T(8,128)}), f32[8,264,128]{2,1,0:T(8,128)S(1)}, u32[]{:S(2)}, u32[]{:S(2)}) async-start(f32[8,264,128]{2,1,0:T(8,128)} %broadcast_in_dim.6), calls=%async_computation.1 | async-start | bytes 2162688 | tf_op jit(solution)/shard_map/columns/all_to_all | solution.py:276
  26.8 13.8 %keys.1 = (bf16[2,1024,512]{2,1,0:T(8,128)(2,1)}, bf16[2,1024,256]{2,1,0:T(8,128)(2,1)}) custom-call(s32[1]{0:T(128)} %bitcast.index, s32[8,128]{1,0:T(8,128)} %bitcast.28, bf16[256,1024]{1,0:T(8,128)(2,1)} %get-tuple-element.34.t1, bf16[256,1024]{1,0:T(8,128)(2,1)} %get-tuple-element.35.t2, bf16[256,1024]{1,0:T(8,128)(2,1)} %get-tuple-element.36.t3, ...), custom_call_target="tpu_custom_call" | custom-call | flops 8000000000 | bytes 10000000 | tf_op jit(solution)/shard_map/keys/pallas_call | solution.py:319
  40.6 0.0 all-to-all-done.1.weights
  40.6 0.0 copy-start.1
  40.6 0.6 slice_bitcast_fusion.ids
  41.2 11.2 %attend.1 = f32[576,128]{1,0:T(8,128)} custom-call(s32[1]{0:T(128)} %bitcast.index, f32[8,128]{1,0:T(8,128)} %slice_bitcast_fusion.ids, f32[512,1024]{1,0:T(8,128)} %get-tuple-element.33.where_sum, bf16[256,1024]{1,0:T(8,128)(2,1)} %get-tuple-element.34.t1, bf16[256,1024]{1,0:T(8,128)(2,1)} %get-tuple-element.35.t2, bf16[256,1024]{1,0:T(8,128)(2,1)} %get-tuple-element.36.t3, ...), custom_call_target="tpu_custom_call" | custom-call | flops 6000000000 | bytes 10000000 | tf_op jit(solution)/shard_map/attend/pallas_call | solution.py:331
  52.4 0.0 copy-done.1
  52.4 8.8 %all-to-all-start.2 = ((f32[64,1,1152]{2,1,0:T(1,128)}), f32[64,1,1152]{2,1,0:T(1,128)S(1)}, u32[]{:S(2)}, u32[]{:S(2)}) async-start(f32[64,1,1152]{2,1,0:T(1,128)} %bitcast.22), calls=%async_computation.2 | async-start | bytes 589824 | tf_op jit(solution)/shard_map/states/all_to_all | solution.py:276
  61.2 2.5 %prepare.1 = (bf16[1024,256]{1,0:T(8,128)(2,1)}, bf16[1024,128]{1,0:T(8,128)(2,1)}, bf16[1024,256]{1,0:T(8,128)(2,1)}) custom-call(f32[8,264,128]{2,1,0:T(8,128)} %copy-done.1), custom_call_target="tpu_custom_call" | custom-call | flops 1000000000 | bytes 3000000 | tf_op jit(solution)/shard_map/prepare/pallas_call | solution.py:347
  63.8 9.1 %all-to-all-done.2 = f32[64,1,1152]{2,1,0:T(1,128)S(1)} async-done(((f32[64,1,1152]{2,1,0:T(1,128)}), f32[64,1,1152]{2,1,0:T(1,128)S(1)}, u32[]{:S(2)}, u32[]{:S(2)}) %all-to-all-start.2) | async-done | bytes 294944 | tf_op jit(solution)/shard_map/states/all_to_all | solution.py:276
  72.8 0.0 copy-start
  72.8 0.7 copy-done
  73.6 2.2 %project.1 = f32[64,128]{1,0:T(8,128)} custom-call(f32[576,128]{1,0:T(8,128)} %bitcast.18, bf16[1024,256]{1,0:T(8,128)(2,1)} %get-tuple-element.42.out_cat), custom_call_target="tpu_custom_call" | custom-call | tf_op jit(solution)/shard_map/project/pallas_call | solution.py:356
  75.8 16.7 %all_to_all.35 = f32[8,8,128]{2,1,0:T(8,128)S(1)} all-to-all(f32[8,8,128]{2,1,0:T(8,128)} %bitcast.24), channel_id=1, replica_groups=mesh['z'=8,'ylo'=2,'x'=4,'yhi'=4,'core'=2] {'yhi','core'}, dimensions={0} | all-to-all | bytes 65536 | tf_op jit(solution)/shard_map/projected/all_to_all | solution.py:276
  92.5 20.5 %all_to_all.36 = f32[64,8,128]{2,1,0:T(8,128)} all-to-all(f32[64,8,128]{2,1,0:T(8,128)S(1)} %broadcast_in_dim.7), channel_id=1, replica_groups=mesh['z'=8,'ylo'=2,'x'=4,'yhi'=4,'core'=2] {'z','yhi','core'}, dimensions={0} | all-to-all | bytes 524288 | tf_op jit(solution)/shard_map/projected/all_to_all | solution.py:276
  113.0 2.6 %latent.1 = f32[512,128]{1,0:T(8,128)} custom-call(f32[512,128]{1,0:T(8,128)} %bitcast.19, bf16[1024,128]{1,0:T(8,128)(2,1)} %get-tuple-element.43.in_cat, bf16[1024,256]{1,0:T(8,128)(2,1)} %get-tuple-element.44.down_cat), custom_call_target="tpu_custom_call" | custom-call | tf_op jit(solution)/shard_map/latent/pallas_call | solution.py:367
  115.6 20.2 %all_to_all.37 = f32[64,8,128]{2,1,0:T(8,128)S(1)} all-to-all(f32[64,8,128]{2,1,0:T(8,128)} %bitcast.20), channel_id=1, replica_groups=mesh['z'=8,'ylo'=2,'x'=4,'yhi'=4,'core'=2] {'z','yhi','core'}, dimensions={0} | all-to-all | bytes 524288 | tf_op jit(solution)/shard_map/result/all_to_all | solution.py:276
  135.8 0.1 reduce_sum.19
  135.9 10.4 %all_to_all.38 = f32[8,8,128]{2,1,0:T(8,128)S(1)} all-to-all(f32[8,8,128]{2,1,0:T(8,128)S(1)} %broadcast_in_dim.8), channel_id=1, replica_groups=mesh['z'=8,'ylo'=2,'x'=4,'yhi'=4,'core'=2] {'yhi','core'}, dimensions={0} | all-to-all | bytes 65536 | tf_op jit(solution)/shard_map/result/all_to_all | solution.py:276
  146.3 0.6 copy.15
  (7 shorter events, 0.1 us)
Async XLA Ops:
  1.6 19.1 %all-to-all-start = ((f32[8,40,128]{2,1,0:T(8,128)}), f32[8,40,128]{2,1,0:T(8,128)S(1)}, u32[]{:S(2)}, u32[]{:S(2)}) async-start(f32[8,40,128]{2,1,0:T(8,128)} %pack.1), calls=%async_computation | async-start | bytes 327680 | tf_op jit(solution)/shard_map/weights/all_to_all | solution.py:276
  21.7 18.8 %all-to-all-start.1 = ((f32[8,264,128]{2,1,0:T(8,128)}), f32[8,264,128]{2,1,0:T(8,128)S(1)}, u32[]{:S(2)}, u32[]{:S(2)}) async-start(f32[8,264,128]{2,1,0:T(8,128)} %broadcast_in_dim.6), calls=%async_computation.1 | async-start | bytes 2162688 | tf_op jit(solution)/shard_map/columns/all_to_all | solution.py:276
  40.6 11.8 %copy-start.1 = (f32[8,264,128]{2,1,0:T(8,128)}, f32[8,264,128]{2,1,0:T(8,128)S(1)}, u32[]{:S(2)}) copy-start(f32[8,264,128]{2,1,0:T(8,128)S(1)} %all-to-all-done.1.weights) | copy-start | bytes 3244036
  52.4 20.4 %all-to-all-start.2 = ((f32[64,1,1152]{2,1,0:T(1,128)}), f32[64,1,1152]{2,1,0:T(1,128)S(1)}, u32[]{:S(2)}, u32[]{:S(2)}) async-start(f32[64,1,1152]{2,1,0:T(1,128)} %bitcast.22), calls=%async_computation.2 | async-start | bytes 589824 | tf_op jit(solution)/shard_map/states/all_to_all | solution.py:276
  72.8 0.7 copy-start

commit v5 on v4

--- a/solution.py
+++ b/solution.py
@@ -15,14 +15,13 @@
 VOCAB = 256
 ROWS_USED = 88
 KEY_STEPS = 1
-LATENT_STEPS = 1
+LATENT_STEPS = 2
 KEY_PARTS = 2
-QUERY_PARTS = 4
+QUERY_PARTS = 1
 
 POS = ("z", "ylo", "x")
 HEAD = ("yhi", "core")
 COLUMN = ("ylo", "x")
-SHARERS = ("z", "yhi", "core")
 
 HIGHEST = lax.Precision.HIGHEST
 NT = (((1,), (1,)), ((), ()))
@@ -241,8 +240,9 @@
     ).astype(jnp.bfloat16)
     both = lax.dot_general(left, out_cat[...], NT, preferred_element_type=jnp.float32)
     partial = both[0:8] + both[8:16]
-    for c in range(8):
-        out[pl.ds(c, 8, stride=8), :] = partial[:, c * 128 : (c + 1) * 128]
+    for copy in range(8):
+        for c in range(8):
+            out[copy, pl.ds(c, 8, stride=8), :] = partial[:, c * 128 : (c + 1) * 128]
 
 
 def latent_kernel(rows, in_cat, down_cat, out):
@@ -357,13 +357,13 @@
         project_kernel,
         in_specs=[VMEM, VMEM],
         out_specs=VMEM,
-        out_shape=shape(64, 128),
+        out_shape=shape(8, 64, 128),
         compiler_params=params(),
         name="project",
     )(states, out_cat)
     with jax.named_scope("projected"):
-        projected = jnp.sum(exchange(partial_rows.reshape(8, 8, 128), HEAD), axis=0)
-        rows = exchange(jnp.broadcast_to(projected[None], (64, 8, 128)), SHARERS)
+        projected = jnp.sum(exchange(partial_rows, HEAD), axis=0)
+        rows = exchange(jnp.broadcast_to(projected[None], (8, 64, 128)), "z")
     outs = pl.pallas_call(
         latent_kernel,
         in_specs=[VMEM] * 3,
@@ -373,8 +373,9 @@
         name="latent",
     )(rows.reshape(512, 128), in_cat, down_cat)
     with jax.named_scope("result"):
-        own = projected + jnp.sum(exchange(outs.reshape(64, 8, 128), SHARERS), axis=0)
-        return exchange(jnp.broadcast_to(own[None], (8, 8, 128)), HEAD).reshape(8, D)
+        own = jnp.sum(exchange(outs.reshape(8, 64, 128), "z"), axis=0)
+        total = jnp.sum(exchange(jnp.broadcast_to(own[None], (8, 64, 128)), HEAD), axis=0)
+        return (projected + total).reshape(8, D)
 
 
 def solution(mesh):

time: 148 us -> 143 us (0.966)
  blocking collectives: 67.8 us -> 63.2 us
    all_to_all x4, blocking collectives: 67.8 us -> 63.2 us  [exchange(): return lax.all_to_all(value, axes, 0, 0)]
where the time goes in v5:
time: 143 us; the launch traced here: 142 us
  blocking collectives  63.2 us (44%)
  Pallas kernels  39.7 us (28%)
  starting transfers between devices  24.7 us (17%)
  waiting for transfers between devices  11.6 us (8%)
  local copies, waits for them, and re-layouts  3.08 us (2%)
    all_to_all x4, blocking collectives, exchange(): return lax.all_to_all(value, axes, 0, 0)  63.2 us
    all_to_all x3, starting transfers between devices, exchange(): return lax.all_to_all(value, axes, 0, 0)  24.7 us
    pallas_call x1, Pallas kernels, per_device(): pl.pallas_call(keys_kernel, grid=(KEY_STEPS,), in_specs=[SMEM, whole(8, 1...  13.8 us
    all_to_all x3, waiting for transfers between devices, exchange(): return lax.all_to_all(value, axes, 0, 0)  11.6 us
    pallas_call x1, Pallas kernels, per_device(): pl.pallas_call(attend_kernel, grid=(LATENT_STEPS,), in_specs=[SMEM, whole...  11.2 us
    pallas_call x1, Pallas kernels, per_device(): pl.pallas_call(tables_kernel, grid=(D // width,), in_specs=[lanes(VOCAB,...  5.75 us
  transfers between devices with their start and end apart: 3, of which 2 were waited for; matrix products, arithmetic and copies ran while one was open for 0% of the time, Pallas kernels for 15%

profile of v5, /device:TPU:1, one launch (start us, length us, event | category | flops | bytes accessed | tf_op | source)
XLA Modules:
  0.0 142.5 jit_solution(15775725167858017031)
XLA Ops:
  0.0 1.6 %pack.1 = f32[8,40,128]{2,1,0:T(8,128)} custom-call(s32[8,128]{1,0:T(8,128)} %bitcast.20, f32[16,128]{1,0:T(8,128)} %bitcast.19, f32[16,512]{1,0:T(8,128)} %w_in.1, f32[16,512]{1,0:T(8,128)} %bitcast.18), custom_call_target="tpu_custom_call" | custom-call | tf_op jit(solution)/shard_map/weights/pack/pallas_call | solution.py:289
  1.6 10.9 %all-to-all-start = ((f32[8,40,128]{2,1,0:T(8,128)}), f32[8,40,128]{2,1,0:T(8,128)S(1)}, u32[]{:S(2)}, u32[]{:S(2)}) async-start(f32[8,40,128]{2,1,0:T(8,128)} %pack.1), calls=%async_computation | async-start | bytes 327680 | tf_op jit(solution)/shard_map/weights/all_to_all | solution.py:276
  12.4 5.7 %tables.1 = (bf16[256,1024]{1,0:T(8,128)(2,1)}, bf16[256,1024]{1,0:T(8,128)(2,1)}, bf16[256,1024]{1,0:T(8,128)(2,1)}, bf16[384,1024]{1,0:T(8,128)(2,1)}, bf16[38...) custom-call(f32[256,1024]{1,0:T(8,128)} %token_.1, f32[256,1024]{1,0:T(8,128)} %row.1, ...), custom_call_target="tpu_custom_call" | custom-call | flops 2000000000 | bytes 8000000 | tf_op jit(solution)/shard_map/tables/pallas_call | solution.py:300
  18.2 2.5 %all-to-all-done = f32[8,40,128]{2,1,0:T(8,128)S(1)} async-done(((f32[8,40,128]{2,1,0:T(8,128)}), f32[8,40,128]{2,1,0:T(8,128)S(1)}, u32[]{:S(2)}, u32[]{:S(2)}) %all-to-all-start) | async-done | bytes 163872 | tf_op jit(solution)/shard_map/weights/all_to_all | solution.py:276
  20.7 1.1 broadcast_in_dim.6
  21.8 5.0 %all-to-all-start.1 = ((f32[8,264,128]{2,1,0:T(8,128)}), f32[8,264,128]{2,1,0:T(8,128)S(1)}, u32[]{:S(2)}, u32[]{:S(2)}) async-start(f32[8,264,128]{2,1,0:T(8,128)} %broadcast_in_dim.6), calls=%async_computation.1 | async-start | bytes 2162688 | tf_op jit(solution)/shard_map/columns/all_to_all | solution.py:276
  26.8 13.8 %keys.1 = (bf16[2,1024,512]{2,1,0:T(8,128)(2,1)}, bf16[2,1024,256]{2,1,0:T(8,128)(2,1)}) custom-call(s32[1]{0:T(128)} %bitcast.index, s32[8,128]{1,0:T(8,128)} %bitcast.21, bf16[256,1024]{1,0:T(8,128)(2,1)} %get-tuple-element.34.t1, bf16[256,1024]{1,0:T(8,128)(2,1)} %get-tuple-element.35.t2, bf16[256,1024]{1,0:T(8,128)(2,1)} %get-tuple-element.36.t3, ...), custom_call_target="tpu_custom_call" | custom-call | flops 8000000000 | bytes 10000000 | tf_op jit(solution)/shard_map/keys/pallas_call | solution.py:319
  40.6 0.0 all-to-all-done.1.weights
  40.6 0.0 copy-start.1
  40.6 0.6 slice_bitcast_fusion.ids
  41.2 11.2 %attend.1 = f32[576,128]{1,0:T(8,128)} custom-call(s32[1]{0:T(128)} %bitcast.index, f32[8,128]{1,0:T(8,128)} %slice_bitcast_fusion.ids, f32[512,1024]{1,0:T(8,128)} %get-tuple-element.33.where_sum, bf16[256,1024]{1,0:T(8,128)(2,1)} %get-tuple-element.34.t1, bf16[256,1024]{1,0:T(8,128)(2,1)} %get-tuple-element.35.t2, bf16[256,1024]{1,0:T(8,128)(2,1)} %get-tuple-element.36.t3, ...), custom_call_target="tpu_custom_call" | custom-call | flops 6000000000 | bytes 10000000 | tf_op jit(solution)/shard_map/attend/pallas_call | solution.py:331
  52.4 0.0 copy-done.1
  52.4 8.8 %all-to-all-start.2 = ((f32[64,1,1152]{2,1,0:T(1,128)}), f32[64,1,1152]{2,1,0:T(1,128)S(1)}, u32[]{:S(2)}, u32[]{:S(2)}) async-start(f32[64,1,1152]{2,1,0:T(1,128)} %bitcast.17), calls=%async_computation.2 | async-start | bytes 589824 | tf_op jit(solution)/shard_map/states/all_to_all | solution.py:276
  61.2 2.5 %prepare.1 = (bf16[1024,256]{1,0:T(8,128)(2,1)}, bf16[1024,128]{1,0:T(8,128)(2,1)}, bf16[1024,256]{1,0:T(8,128)(2,1)}) custom-call(f32[8,264,128]{2,1,0:T(8,128)} %copy-done.1), custom_call_target="tpu_custom_call" | custom-call | flops 1000000000 | bytes 3000000 | tf_op jit(solution)/shard_map/prepare/pallas_call | solution.py:347
  63.7 9.1 %all-to-all-done.2 = f32[64,1,1152]{2,1,0:T(1,128)S(1)} async-done(((f32[64,1,1152]{2,1,0:T(1,128)}), f32[64,1,1152]{2,1,0:T(1,128)S(1)}, u32[]{:S(2)}, u32[]{:S(2)}) %all-to-all-start.2) | async-done | bytes 294944 | tf_op jit(solution)/shard_map/states/all_to_all | solution.py:276
  72.8 0.0 copy-start
  72.8 0.7 copy-done
  73.6 2.3 %project.1 = f32[8,64,128]{2,1,0:T(8,128)} custom-call(f32[576,128]{1,0:T(8,128)} %bitcast.13, bf16[1024,256]{1,0:T(8,128)(2,1)} %get-tuple-element.42.out_cat), custom_call_target="tpu_custom_call" | custom-call | tf_op jit(solution)/shard_map/project/pallas_call | solution.py:356
  75.9 19.4 %all_to_all.35 = f32[8,64,128]{2,1,0:T(8,128)S(1)} all-to-all(f32[8,64,128]{2,1,0:T(8,128)} %project.1), channel_id=1, replica_groups=mesh['z'=8,'ylo'=2,'x'=4,'yhi'=4,'core'=2] {'yhi','core'}, dimensions={0} | all-to-all | bytes 524288 | tf_op jit(solution)/shard_map/projected/all_to_all | solution.py:276
  95.4 12.5 %all_to_all.36 = f32[8,64,128]{2,1,0:T(8,128)} all-to-all(f32[8,64,128]{2,1,0:T(8,128)S(1)} %broadcast_in_dim.7), channel_id=1, replica_groups=mesh['z'=8,'ylo'=2,'x'=4,'yhi'=4,'core'=2] {'z'}, dimensions={0} | all-to-all | bytes 524288 | tf_op jit(solution)/shard_map/projected/all_to_all | solution.py:276
  107.8 2.6 %latent.1 = f32[512,128]{1,0:T(8,128)} custom-call(f32[512,128]{1,0:T(8,128)} %bitcast.14, bf16[1024,128]{1,0:T(8,128)(2,1)} %get-tuple-element.43.in_cat, bf16[1024,256]{1,0:T(8,128)(2,1)} %get-tuple-element.44.down_cat), custom_call_target="tpu_custom_call" | custom-call | tf_op jit(solution)/shard_map/latent/pallas_call | solution.py:367
  110.4 12.7 %all_to_all.37 = f32[8,64,128]{2,1,0:T(8,128)S(1)} all-to-all(f32[8,64,128]{2,1,0:T(8,128)} %bitcast.15), channel_id=1, replica_groups=mesh['z'=8,'ylo'=2,'x'=4,'yhi'=4,'core'=2] {'z'}, dimensions={0} | all-to-all | bytes 524288 | tf_op jit(solution)/shard_map/result/all_to_all | solution.py:276
  123.2 18.6 %all_to_all.38 = f32[8,64,128]{2,1,0:T(8,128)S(1)} all-to-all(f32[8,64,128]{2,1,0:T(8,128)S(1)} %broadcast_in_dim.8), channel_id=1, replica_groups=mesh['z'=8,'ylo'=2,'x'=4,'yhi'=4,'core'=2] {'yhi','core'}, dimensions={0} | all-to-all | bytes 524288 | tf_op jit(solution)/shard_map/result/all_to_all | solution.py:276
  141.8 0.6 add.16
  (9 shorter events, 0.1 us)
Async XLA Ops:
  1.6 19.1 %all-to-all-start = ((f32[8,40,128]{2,1,0:T(8,128)}), f32[8,40,128]{2,1,0:T(8,128)S(1)}, u32[]{:S(2)}, u32[]{:S(2)}) async-start(f32[8,40,128]{2,1,0:T(8,128)} %pack.1), calls=%async_computation | async-start | bytes 327680 | tf_op jit(solution)/shard_map/weights/all_to_all | solution.py:276
  21.8 18.8 %all-to-all-start.1 = ((f32[8,264,128]{2,1,0:T(8,128)}), f32[8,264,128]{2,1,0:T(8,128)S(1)}, u32[]{:S(2)}, u32[]{:S(2)}) async-start(f32[8,264,128]{2,1,0:T(8,128)} %broadcast_in_dim.6), calls=%async_computation.1 | async-start | bytes 2162688 | tf_op jit(solution)/shard_map/columns/all_to_all | solution.py:276
  40.6 11.8 %copy-start.1 = (f32[8,264,128]{2,1,0:T(8,128)}, f32[8,264,128]{2,1,0:T(8,128)S(1)}, u32[]{:S(2)}) copy-start(f32[8,264,128]{2,1,0:T(8,128)S(1)} %all-to-all-done.1.weights) | copy-start | bytes 3244036
  52.4 20.4 %all-to-all-start.2 = ((f32[64,1,1152]{2,1,0:T(1,128)}), f32[64,1,1152]{2,1,0:T(1,128)S(1)}, u32[]{:S(2)}, u32[]{:S(2)}) async-start(f32[64,1,1152]{2,1,0:T(1,128)} %bitcast.17), calls=%async_computation.2 | async-start | bytes 589824 | tf_op jit(solution)/shard_map/states/all_to_all | solution.py:276
  72.8 0.7 copy-start
